TPU v7x, 32 devices: a whole 2x2x4 slice. The times are simulated.
32 devices in a mesh: row: 8 (over z, core), sample: 4 (over y, x).
Axes of the slice: x: 2, y: 2, z: 4, core: 2. Of those that a mesh axis runs over, the one named last changes fastest.
Arguments:
- tokens: bfloat16 [2, 12, 512, 768], P(None, 'sample', 'row'), may hold values from -6 to 6
- single: bfloat16 [2, 12, 512, 384], P(None, 'sample', 'row'), may hold values from -6 to 6
- pair: bfloat16 [2, 512, 512, 128], P(None, 'row'), may hold values from -6 to 6
- token_count: int32 [2], replicated, may hold values from 256 to 512, as said below
- pair_mask: int32 [2, 512, 512], P(None, 'row'), may hold values 0 or 1
- cotangent: bfloat16 [2, 12, 512, 768], P(None, 'sample', 'row'), may hold values from -6 to 6
- cond_gain: bfloat16 [2, 384], P(None, 'sample'), may hold values from 0.5 to 1.5
- ada_weight: bfloat16 [4, 384, 768], P(None, 'sample'), may hold values from -0.3125 to 0.3125
- ada_bias: bfloat16 [2, 768], P(None, 'sample'), may hold values from -3 to 3
- zero_weight: bfloat16 [2, 384, 768], P(None, 'sample'), may hold values from -0.3125 to 0.3125
- zero_bias: bfloat16 [2, 768], P(None, 'sample'), may hold values from -4 to 4
- attn_weight: bfloat16 [4, 768, 768], P(None, 'sample'), may hold values from -0.21875 to 0.21875
- query_bias: bfloat16 [768], P('sample'), may hold values from -3 to 3
- out_weight: bfloat16 [768, 768], P('sample'), may hold values from -1.75 to 1.75
- pair_gain: bfloat16 [128], P('sample'), may hold values from 0.25 to 1.75
- pair_weight: bfloat16 [128, 16], P('sample'), may hold values from -0.5 to 0.5
- trans_in: bfloat16 [2, 768, 1536], P(None, 'sample'), may hold values from -0.21875 to 0.21875
- trans_out: bfloat16 [1536, 768], P('sample'), may hold values from -0.3125 to 0.3125
Outputs:
- output: bfloat16 [2, 12, 512, 768], P(None, 'sample', 'row')
- token_grad: float32 [2, 12, 512, 768], P(None, 'sample', 'row')
- cond_gain_grad: float32 [2, 384], P(None, 'sample')
- ada_weight_grad: float32 [4, 384, 768], P(None, 'sample')
- ada_bias_grad: float32 [2, 768], P(None, 'sample')
- zero_weight_grad: float32 [2, 384, 768], P(None, 'sample')
- zero_bias_grad: float32 [2, 768], P(None, 'sample')
- attn_weight_grad: float32 [4, 768, 768], P(None, 'sample')
- query_bias_grad: float32 [768], P('sample')
- out_weight_grad: float32 [768, 768], P('sample')
- pair_gain_grad: float32 [128], P('sample')
- pair_weight_grad: float32 [128, 16], P('sample')
- trans_in_grad: float32 [2, 768, 1536], P(None, 'sample')
- trans_out_grad: float32 [1536, 768], P('sample')
Inputs may be any that keep to these rules, and one draw needn't show every extreme that they name: The tokens of complex c are the positions below token_count[c], the rest is padding; each count is 256 or more, and in every draw one complex, at a drawn place, has all 512 tokens.
All inputs are finite; a program needn't handle non-finite values. No bound on the sum of `pair_mask` on one device may be relied on, other than what follows from the above.
Results may differ from a plain program's by a relative error of at most 0.023.
Values may be sent and summed in bfloat16 or wider, within the bound.
A program may use at most 256 MiB of HBM per device.

v0:
```python
import jax
import jax.numpy as jnp
from jax import lax
from jax.sharding import PartitionSpec as P

EPSILON = 1e-05
MASKED = -1000000000.0
HIGHEST = lax.Precision.HIGHEST
FULL_TYPE = jnp.float32
HALF_TYPE = jnp.bfloat16


def norm_rows(value):
    center = value - jnp.mean(value, axis=-1, keepdims=True)
    return center * lax.rsqrt(jnp.mean(center * center, axis=-1, keepdims=True) + EPSILON)


def adaptive_tail(activation, gate_pre, shift_value):
    return jax.nn.sigmoid(gate_pre) * norm_rows(activation) + shift_value


def rows_dot(left, right):
    return jnp.dot(left, right, preferred_element_type=FULL_TYPE)


def back_dot(grad_rows, weight):
    return jnp.dot(grad_rows, weight.T, preferred_element_type=FULL_TYPE)


def weight_grad(left, grad_rows):
    flat_left = left.reshape(-1, left.shape[-1])
    flat_grad = grad_rows.reshape(-1, grad_rows.shape[-1])
    return jnp.einsum("ta,tb->ab", flat_left, flat_grad, preferred_element_type=FULL_TYPE)


def row_total(grad_rows):
    return jnp.sum(grad_rows.astype(FULL_TYPE).reshape(-1, grad_rows.shape[-1]), axis=0)


def layer_pass(weights, token_in, cond_in, pair_in, count_now, mask_in, cot_in, own_pos, key_pos):
    (
        cond_gains,
        ada_weights,
        ada_biases,
        zero_weights,
        zero_biases,
        attn_weights,
        query_biases,
        out_weights,
        pair_gains,
        pair_weights,
        trans_ins,
        trans_outs,
    ) = weights
    samp_dev, rows_dev, width = token_in.shape
    length = key_pos.shape[0]
    heads = pair_weights.shape[1]
    head_dim = width // heads
    scale = head_dim ** (-0.5)
    valid_rows = (own_pos < count_now).astype(FULL_TYPE)[None, :, None]
    allowed = (key_pos[None, :] < count_now) & (
        (mask_in == 1) | (own_pos[:, None] == key_pos[None, :]) | (own_pos[:, None] >= count_now)
    )
    pair_normed = norm_rows(pair_in.astype(FULL_TYPE))
    pair_low = (pair_normed * pair_gains.astype(FULL_TYPE)).astype(HALF_TYPE)
    bias = jnp.einsum("ijc,ch->hij", pair_low, pair_weights, preferred_element_type=FULL_TYPE)
    token_full = token_in.astype(FULL_TYPE)
    cond_normed = norm_rows(cond_in.astype(FULL_TYPE))
    attn_cond = (cond_normed * cond_gains[0].astype(FULL_TYPE)).astype(HALF_TYPE)
    attn_pre = rows_dot(attn_cond, ada_weights[0]) + ada_biases[0].astype(FULL_TYPE)
    attn_shift = rows_dot(attn_cond, ada_weights[1])
    normed_in = adaptive_tail(token_full, attn_pre, attn_shift).astype(HALF_TYPE)
    queries = (rows_dot(normed_in, attn_weights[0]) + query_biases.astype(FULL_TYPE)).astype(
        HALF_TYPE
    )
    gate_value = jax.nn.sigmoid(rows_dot(normed_in, attn_weights[3]))
    key_rows = rows_dot(normed_in, attn_weights[1]).astype(HALF_TYPE)
    value_rows = rows_dot(normed_in, attn_weights[2]).astype(HALF_TYPE)
    key_all, value_all = (
        lax.all_gather(key_rows, "row", axis=1, tiled=True),
        lax.all_gather(value_rows, "row", axis=1, tiled=True),
    )
    query_heads = queries.reshape(samp_dev, rows_dev, heads, head_dim)
    key_heads = key_all.reshape(samp_dev, length, heads, head_dim)
    value_heads = value_all.reshape(samp_dev, length, heads, head_dim)

    def scores_of():
        raw = jnp.einsum(
            "nihd,njhd->nhij", query_heads, key_heads, preferred_element_type=FULL_TYPE
        )
        return jnp.where(allowed[None, None], raw * scale + bias[None], MASKED)

    scores = scores_of()
    top_score = jnp.max(scores, axis=-1, keepdims=True)
    log_total = top_score + jnp.log(jnp.sum(jnp.exp(scores - top_score), axis=-1, keepdims=True))
    attn_prob = jnp.exp(scores - log_total)
    attended = jnp.einsum(
        "nhij,njhd->nihd",
        attn_prob.astype(HALF_TYPE),
        value_heads,
        preferred_element_type=FULL_TYPE,
    ).reshape(samp_dev, rows_dev, width)
    gated = (attended * gate_value).astype(HALF_TYPE)
    attn_branch = rows_dot(gated, out_weights)
    attn_zero = jax.nn.sigmoid(
        rows_dot(cond_in, zero_weights[0]) + zero_biases[0].astype(FULL_TYPE)
    )
    middle = token_full + valid_rows * attn_zero * attn_branch
    trans_cond = (cond_normed * cond_gains[1].astype(FULL_TYPE)).astype(HALF_TYPE)
    trans_pre = rows_dot(trans_cond, ada_weights[2]) + ada_biases[1].astype(FULL_TYPE)
    trans_shift = rows_dot(trans_cond, ada_weights[3])
    trans_input = adaptive_tail(middle, trans_pre, trans_shift).astype(HALF_TYPE)
    first_proj = rows_dot(trans_input, trans_ins[0])
    second_proj = rows_dot(trans_input, trans_ins[1])
    hidden = (jax.nn.silu(first_proj) * second_proj).astype(HALF_TYPE)
    trans_branch = rows_dot(hidden, trans_outs)
    trans_zero = jax.nn.sigmoid(
        rows_dot(cond_in, zero_weights[1]) + zero_biases[1].astype(FULL_TYPE)
    )
    result = (middle + valid_rows * trans_zero * trans_branch).astype(HALF_TYPE)
    grad_out = cot_in.astype(FULL_TYPE)
    grad_tbranch = (grad_out * valid_rows * trans_zero).astype(HALF_TYPE)
    grad_zlogit_b = (grad_out * valid_rows * trans_branch * trans_zero * (1.0 - trans_zero)).astype(
        HALF_TYPE
    )
    grad_hidden = back_dot(grad_tbranch, trans_outs)
    sig_first = jax.nn.sigmoid(first_proj)
    grad_first = (
        grad_hidden * second_proj * sig_first * (1.0 + first_proj * (1.0 - sig_first))
    ).astype(HALF_TYPE)
    grad_second = (grad_hidden * first_proj * sig_first).astype(HALF_TYPE)
    grad_tin = (back_dot(grad_first, trans_ins[0]) + back_dot(grad_second, trans_ins[1])).astype(
        HALF_TYPE
    )
    trans_tail, trans_pull = jax.vjp(adaptive_tail, middle, trans_pre, trans_shift)
    grad_mid_tail, grad_tpre, shift_grad = trans_pull(grad_tin.astype(FULL_TYPE))
    grad_tpre = grad_tpre.astype(HALF_TYPE)
    grad_tcond = back_dot(grad_tpre, ada_weights[2]) + back_dot(grad_tin, ada_weights[3])
    grad_middle = grad_out + grad_mid_tail
    grad_abranch = (grad_middle * valid_rows * attn_zero).astype(HALF_TYPE)
    grad_zlogit_a = (grad_middle * valid_rows * attn_branch * attn_zero * (1.0 - attn_zero)).astype(
        HALF_TYPE
    )
    grad_gated = back_dot(grad_abranch, out_weights)
    grad_attended = (grad_gated * gate_value).astype(HALF_TYPE)
    grad_glogit = (grad_gated * attended * gate_value * (1.0 - gate_value)).astype(HALF_TYPE)
    grad_heads = grad_attended.reshape(samp_dev, rows_dev, heads, head_dim)
    again_scores = scores_of()
    again_prob = jnp.exp(again_scores - log_total)
    grad_prob = jnp.einsum(
        "nihd,njhd->nhij", grad_heads, value_heads, preferred_element_type=FULL_TYPE
    )
    row_inner = jnp.sum(grad_prob * again_prob, axis=-1, keepdims=True)
    grad_scores = (again_prob * (grad_prob - row_inner)).astype(HALF_TYPE)
    grad_query = (
        (
            jnp.einsum("nhij,njhd->nihd", grad_scores, key_heads, preferred_element_type=FULL_TYPE)
            * scale
        )
        .reshape(samp_dev, rows_dev, width)
        .astype(HALF_TYPE)
    )
    grad_bias = jnp.sum(grad_scores.astype(FULL_TYPE), axis=0)
    grad_value = jnp.einsum(
        "nhij,nihd->njhd",
        again_prob.astype(HALF_TYPE),
        grad_heads,
        preferred_element_type=FULL_TYPE,
    ).reshape(samp_dev, length, width)
    grad_key = (
        jnp.einsum("nhij,nihd->njhd", grad_scores, query_heads, preferred_element_type=FULL_TYPE)
        * scale
    ).reshape(samp_dev, length, width)
    grad_key_own, grad_value_own = (
        lax.psum_scatter(grad_key, "row", scatter_dimension=1, tiled=True),
        lax.psum_scatter(grad_value, "row", scatter_dimension=1, tiled=True),
    )
    grad_key_low = grad_key_own.astype(HALF_TYPE)
    grad_value_low = grad_value_own.astype(HALF_TYPE)
    grad_normed = (
        back_dot(grad_query, attn_weights[0])
        + back_dot(grad_key_low, attn_weights[1])
        + back_dot(grad_value_low, attn_weights[2])
        + back_dot(grad_glogit, attn_weights[3])
    ).astype(HALF_TYPE)
    attn_tail, attn_pull = jax.vjp(adaptive_tail, token_full, attn_pre, attn_shift)
    grad_token_tail, grad_apre, shift_grad_attn = attn_pull(grad_normed.astype(FULL_TYPE))
    grad_apre = grad_apre.astype(HALF_TYPE)
    grad_acond = back_dot(grad_apre, ada_weights[0]) + back_dot(grad_normed, ada_weights[1])
    token_grad = grad_middle + grad_token_tail
    grad_pair_low = jnp.einsum(
        "hij,ch->ijc", grad_bias, pair_weights.astype(FULL_TYPE), precision=HIGHEST
    )
    pair_weight_grad = jnp.einsum(
        "ijc,hij->ch", pair_low.astype(FULL_TYPE), grad_bias, precision=HIGHEST
    )
    pair_gain_grad = jnp.sum(grad_pair_low * pair_normed, axis=(0, 1))
    cond_gain_grad = jnp.stack(
        [
            jnp.sum(grad_acond * cond_normed, axis=(0, 1)),
            jnp.sum(grad_tcond * cond_normed, axis=(0, 1)),
        ]
    )
    ada_weight_grad = jnp.stack(
        [
            weight_grad(attn_cond, grad_apre),
            weight_grad(attn_cond, grad_normed),
            weight_grad(trans_cond, grad_tpre),
            weight_grad(trans_cond, grad_tin),
        ]
    )
    ada_bias_grad = jnp.stack([row_total(grad_apre), row_total(grad_tpre)])
    zero_weight_grad = jnp.stack(
        [weight_grad(cond_in, grad_zlogit_a), weight_grad(cond_in, grad_zlogit_b)]
    )
    zero_bias_grad = jnp.stack([row_total(grad_zlogit_a), row_total(grad_zlogit_b)])
    attn_weight_grad = jnp.stack(
        [
            weight_grad(normed_in, grad_query),
            weight_grad(normed_in, grad_key_low),
            weight_grad(normed_in, grad_value_low),
            weight_grad(normed_in, grad_glogit),
        ]
    )
    query_bias_grad = row_total(grad_query)
    out_weight_grad = weight_grad(gated, grad_abranch)
    trans_in_grad = jnp.stack(
        [weight_grad(trans_input, grad_first), weight_grad(trans_input, grad_second)]
    )
    trans_out_grad = weight_grad(hidden, grad_tbranch)
    grads = (
        cond_gain_grad,
        ada_weight_grad,
        ada_bias_grad,
        zero_weight_grad,
        zero_bias_grad,
        attn_weight_grad,
        query_bias_grad,
        out_weight_grad,
        pair_gain_grad,
        pair_weight_grad,
        trans_in_grad,
        trans_out_grad,
    )
    return (result, token_grad, grads)


def local(
    tokens,
    single,
    pair,
    token_count,
    pair_mask,
    cotangent,
    cond_gain,
    ada_weight,
    ada_bias,
    zero_weight,
    zero_bias,
    attn_weight,
    query_bias,
    out_weight,
    pair_gain,
    pair_weight,
    trans_in,
    trans_out,
):
    rows_dev = tokens.shape[2]
    length = pair.shape[2]
    own_pos = lax.axis_index("row") * rows_dev + jnp.arange(rows_dev, dtype=jnp.int32)
    key_pos = jnp.arange(length, dtype=jnp.int32)
    shards = (
        cond_gain,
        ada_weight,
        ada_bias,
        zero_weight,
        zero_bias,
        attn_weight,
        query_bias,
        out_weight,
        pair_gain,
        pair_weight,
        trans_in,
        trans_out,
    )
    start = tuple((jnp.zeros(piece.shape, FULL_TYPE) for piece in shards))

    def one_batch(carry, inputs):
        token_now, single_now, pair_now, count_now, mask_now, cot_now = inputs
        gathered = (
            lax.all_gather(cond_gain, "sample", axis=1, tiled=True),
            lax.all_gather(ada_weight, "sample", axis=1, tiled=True),
            lax.all_gather(ada_bias, "sample", axis=1, tiled=True),
            lax.all_gather(zero_weight, "sample", axis=1, tiled=True),
            lax.all_gather(zero_bias, "sample", axis=1, tiled=True),
            lax.all_gather(attn_weight, "sample", axis=1, tiled=True),
            lax.all_gather(query_bias, "sample", axis=0, tiled=True),
            lax.all_gather(out_weight, "sample", axis=0, tiled=True),
            lax.all_gather(pair_gain, "sample", axis=0, tiled=True),
            lax.all_gather(pair_weight, "sample", axis=0, tiled=True),
            lax.all_gather(trans_in, "sample", axis=1, tiled=True),
            lax.all_gather(trans_out, "sample", axis=0, tiled=True),
        )
        result, token_grad, grads = layer_pass(
            gathered,
            token_now,
            single_now,
            pair_now,
            count_now,
            mask_now,
            cot_now,
            own_pos,
            key_pos,
        )
        shard_part = (
            lax.psum_scatter(
                grads[0].astype(jnp.bfloat16), "sample", scatter_dimension=1, tiled=True
            ).astype(jnp.float32),
            lax.psum_scatter(
                grads[1].astype(jnp.bfloat16), "sample", scatter_dimension=1, tiled=True
            ).astype(jnp.float32),
            lax.psum_scatter(
                grads[2].astype(jnp.bfloat16), "sample", scatter_dimension=1, tiled=True
            ).astype(jnp.float32),
            lax.psum_scatter(
                grads[3].astype(jnp.bfloat16), "sample", scatter_dimension=1, tiled=True
            ).astype(jnp.float32),
            lax.psum_scatter(
                grads[4].astype(jnp.bfloat16), "sample", scatter_dimension=1, tiled=True
            ).astype(jnp.float32),
            lax.psum_scatter(
                grads[5].astype(jnp.bfloat16), "sample", scatter_dimension=1, tiled=True
            ).astype(jnp.float32),
            lax.psum_scatter(
                grads[6].astype(jnp.bfloat16), "sample", scatter_dimension=0, tiled=True
            ).astype(jnp.float32),
            lax.psum_scatter(
                grads[7].astype(jnp.bfloat16), "sample", scatter_dimension=0, tiled=True
            ).astype(jnp.float32),
            lax.psum_scatter(
                grads[8].astype(jnp.bfloat16), "sample", scatter_dimension=0, tiled=True
            ).astype(jnp.float32),
            lax.psum_scatter(
                grads[9].astype(jnp.bfloat16), "sample", scatter_dimension=0, tiled=True
            ).astype(jnp.float32),
            lax.psum_scatter(
                grads[10].astype(jnp.bfloat16), "sample", scatter_dimension=1, tiled=True
            ).astype(jnp.float32),
            lax.psum_scatter(
                grads[11].astype(jnp.bfloat16), "sample", scatter_dimension=0, tiled=True
            ).astype(jnp.float32),
        )
        carry = tuple((running + update for running, update in zip(carry, shard_part)))
        return (carry, (result, token_grad))

    totals, stacked = lax.scan(
        one_batch, start, (tokens, single, pair, token_count, pair_mask, cotangent)
    )
    summed = (
        lax.psum(totals[0].astype(jnp.bfloat16), "row").astype(jnp.float32),
        lax.psum(totals[1].astype(jnp.bfloat16), "row").astype(jnp.float32),
        lax.psum(totals[2].astype(jnp.bfloat16), "row").astype(jnp.float32),
        lax.psum(totals[3].astype(jnp.bfloat16), "row").astype(jnp.float32),
        lax.psum(totals[4].astype(jnp.bfloat16), "row").astype(jnp.float32),
        lax.psum(totals[5].astype(jnp.bfloat16), "row").astype(jnp.float32),
        lax.psum(totals[6].astype(jnp.bfloat16), "row").astype(jnp.float32),
        lax.psum(totals[7].astype(jnp.bfloat16), "row").astype(jnp.float32),
        lax.psum(totals[8].astype(jnp.bfloat16), "row").astype(jnp.float32),
        lax.psum(totals[9].astype(jnp.bfloat16), "row").astype(jnp.float32),
        lax.psum(totals[10].astype(jnp.bfloat16), "row").astype(jnp.float32),
        lax.psum(totals[11].astype(jnp.bfloat16), "row").astype(jnp.float32),
    )
    return (
        stacked[0],
        stacked[1],
        summed[0],
        summed[1],
        summed[2],
        summed[3],
        summed[4],
        summed[5],
        summed[6],
        summed[7],
        summed[8],
        summed[9],
        summed[10],
        summed[11],
    )


def solution(mesh):
    return jax.shard_map(
        local,
        mesh=mesh,
        in_specs=(
            P(None, "sample", "row", None),
            P(None, "sample", "row", None),
            P(None, "row", None, None),
            P(),
            P(None, "row", None),
            P(None, "sample", "row", None),
            P(None, "sample"),
            P(None, "sample", None),
            P(None, "sample"),
            P(None, "sample", None),
            P(None, "sample"),
            P(None, "sample", None),
            P("sample"),
            P("sample", None),
            P("sample"),
            P("sample", None),
            P(None, "sample", None),
            P("sample", None),
        ),
        out_specs=(
            P(None, "sample", "row", None),
            P(None, "sample", "row", None),
            P(None, "sample"),
            P(None, "sample", None),
            P(None, "sample"),
            P(None, "sample", None),
            P(None, "sample"),
            P(None, "sample", None),
            P("sample"),
            P("sample", None),
            P("sample"),
            P("sample", None),
            P(None, "sample", None),
            P("sample", None),
        ),
        check_vma=False,
    )
```

profile of v0, /device:TPU:0, one launch (start us, length us, event | category | flops | bytes accessed | tf_op | source)
XLA Modules:
  0.0 1810.4 jit_solution(8889101236310632782)
XLA Ops:
  8.2 1678.6 %while.38 = (s32[]{:T(128)}, f32[2,96]{1,0:T(2,128)}, f32[4,96,768]{2,1,0:T(8,128)}, f32[2,192]{1,0:T(2,128)}, f32[2,96,768]{2,1,0:T(8,128)}, /*index=5*/f32[2,1...) while((s32[]{:T(128)}, f32[2,96]{1,0:T(2,128)}, ...), condition=%wide.region_39.40_spmd.clone.clone, body=%wide.region_0.39_spmd.clone.clone.sunk | while | flops 12116579328 | bytes 722232384 | solution.py:356
  10.7 9.5 all-gather.13
  20.3 7.9 all-gather.12
  30.1 21.4 %all-gather.25.cloned.1.call-done = bf16[4,384,768]{2,1,0:T(8,128)(2,1)} async-done(((bf16[4,96,768]{2,1,0:T(8,128)(2,1)}), bf16[4,384,768]{2,1,0:T(8,128)(2,1)}) %all-gather.25.cloned.1.call-update) | async-done | bytes 2359312 | tf_op jit(solution)/shard_map/while/body/eval_jaxpr/all_gather | solution.py:292
  55.3 55.3 %all-gather.29.cloned.1.call-done = bf16[4,768,768]{2,1,0:T(8,128)(2,1)} async-done(((bf16[4,192,768]{2,1,0:T(8,128)(2,1)}), bf16[4,768,768]{2,1,0:T(8,128)(2,1)}) %all-gather.29.cloned.1.call-update) | async-done | bytes 4718608 | tf_op jit(solution)/shard_map/while/body/eval_jaxpr/all_gather | solution.py:296
  122.0 8.9 all-reduce.12
  131.0 8.0 all-gather.14
  139.1 7.5 all-gather.15
  146.7 5.9 convert_reduce_fusion.10
  152.6 10.8 fusion.431
  163.5 12.9 fusion.432
  190.8 15.1 all-gather.31.cloned.1.call-done
  224.3 10.3 all-gather.35.cloned.1.call-done
  240.1 53.7 %all-gather.37.cloned.1.call-done = bf16[2,768,1536]{2,1,0:T(8,128)(2,1)} async-done(((bf16[2,192,1536]{2,1,0:T(8,128)(2,1)}), bf16[2,768,1536]{2,1,0:T(8,128)(2,1)}) %all-gather.37.cloned.1.call-update) | async-done | bytes 4718608 | tf_op jit(solution)/shard_map/while/body/eval_jaxpr/all_gather | solution.py:301
  297.1 36.2 %all-gather.39.cloned.1.call-done = bf16[1536,768]{1,0:T(8,128)(2,1)} async-done(((bf16[384,768]{1,0:T(8,128)(2,1)}), bf16[1536,768]{1,0:T(8,128)(2,1)}) %all-gather.39.cloned.1.call-update) | async-done | bytes 2359312 | tf_op jit(solution)/shard_map/while/body/eval_jaxpr/all_gather | solution.py:302
  347.2 4.3 multiply_reduce_fusion.8
  358.2 6.0 copy.136
  364.3 6.2 fusion.448
  370.5 6.1 copy.137
  377.3 4.4 fusion.456
  382.6 14.5 fusion.465
  429.9 45.1 %reduce-scatter.31.cloned.1.call-done = f32[3,64,768]{2,1,0:T(8,128)} async-done(((f32[3,512,768]{2,1,0:T(8,128)}), f32[3,64,768]{2,1,0:T(8,128)}) %reduce-scatter.31.cloned.1.call-update) | async-done | bytes 589840 | tf_op jit(solution)/shard_map/while/body/eval_jaxpr/reduce_scatter | solution.py:176
  495.7 24.1 %fusion.463 = bf16[128]{0:T(256)(128)(2,1)S(1)} fusion(bf16[128,16,1]{0,1,2:T(8,128)(2,1)S(1)} %copy-done.89, f32[64,512]{1,0:T(8,128)S(1)} %copy-done.57, f32[64,512]{1,0:T(8,128)S(1)} %copy-done.51, bf16[2,64,512,128]{3,2,1,0:T(8,128)(2,1)} %get-tuple-element.946, s32[]{:T(128)S(6)} %copy.165, f32[16,64,512]{2,1,0:T(8,128)} %get-tuple-element.831), kind=kOutput, calls=%fused_computation.10.clone.1 | convolution fusion | flops 826277760 | bytes 10752260 | tf_op jit(solution)/shard_map/while/body/eval_jaxpr/hij,ch->ijc/dot_general | solution.py:191
  519.8 9.8 all-reduce.13
  532.5 25.7 %reduce-scatter.39.cloned.1.call-done = bf16[2,96,768]{2,1,0:T(8,128)(2,1)} async-done(((bf16[2,384,768]{2,1,0:T(8,128)(2,1)}), bf16[2,96,768]{2,1,0:T(8,128)(2,1)}) %reduce-scatter.39.cloned.1.call-update) | async-done | bytes 294928 | tf_op jit(solution)/shard_map/while/body/eval_jaxpr/reduce_scatter | solution.py:325
  560.0 29.5 %reduce-scatter.45.cloned.1.call-done = bf16[192,768]{1,0:T(8,128)(2,1)} async-done(((bf16[768,768]{1,0:T(8,128)(2,1)}), bf16[192,768]{1,0:T(8,128)(2,1)}) %reduce-scatter.45.cloned.1.call-update) | async-done | bytes 294928 | tf_op jit(solution)/shard_map/while/body/eval_jaxpr/reduce_scatter | solution.py:337
  591.4 38.5 %reduce-scatter.51.cloned.1.call-done = bf16[384,768]{1,0:T(8,128)(2,1)} async-done(((bf16[1536,768]{1,0:T(8,128)(2,1)}), bf16[384,768]{1,0:T(8,128)(2,1)}) %reduce-scatter.51.cloned.1.call-update) | async-done | bytes 589840 | tf_op jit(solution)/shard_map/while/body/eval_jaxpr/reduce_scatter | solution.py:349
  633.9 55.9 %reduce-scatter.49.cloned.1.call-done = bf16[2,192,1536]{2,1,0:T(8,128)(2,1)} async-done(((bf16[2,768,1536]{2,1,0:T(8,128)(2,1)}), bf16[2,192,1536]{2,1,0:T(8,128)(2,1)}) %reduce-scatter.49.cloned.1.call-update) | async-done | bytes 1179664 | tf_op jit(solution)/shard_map/while/body/eval_jaxpr/reduce_scatter | solution.py:346
  693.0 23.2 %reduce-scatter.33.cloned.1.call-done = bf16[96,2]{1,0:T(8,128)(2,1)} async-done(((bf16[384,2]{1,0:T(8,128)(2,1)}), bf16[96,2]{1,0:T(8,128)(2,1)}) %reduce-scatter.33.cloned.1.call-update) | async-done | bytes 400 | tf_op jit(solution)/shard_map/while
  717.1 26.0 %reduce-scatter.37.cloned.1.call-done = bf16[192,2]{1,0:T(8,128)(2,1)} async-done(((bf16[768,2]{1,0:T(8,128)(2,1)}), bf16[192,2]{1,0:T(8,128)(2,1)}) %reduce-scatter.37.cloned.1.call-update) | async-done | bytes 784 | tf_op jit(solution)/shard_map/while
  744.0 39.9 %reduce-scatter.35.cloned.1.call-done = bf16[4,96,768]{2,1,0:T(8,128)(2,1)} async-done(((bf16[4,384,768]{2,1,0:T(8,128)(2,1)}), bf16[4,96,768]{2,1,0:T(8,128)(2,1)}) %reduce-scatter.35.cloned.1.call-update) | async-done | bytes 589840 | tf_op jit(solution)/shard_map/while/body/eval_jaxpr/reduce_scatter | solution.py:319
  785.2 58.8 %reduce-scatter.43.cloned.1.call-done = bf16[4,192,768]{2,1,0:T(8,128)(2,1)} async-done(((bf16[4,768,768]{2,1,0:T(8,128)(2,1)}), bf16[4,192,768]{2,1,0:T(8,128)(2,1)}) %reduce-scatter.43.cloned.1.call-update) | async-done | bytes 1179664 | tf_op jit(solution)/shard_map/while/body/eval_jaxpr/reduce_scatter | solution.py:331
  850.0 7.8 all-gather.13
  857.8 7.2 all-gather.12
  866.9 21.1 %all-gather.25.cloned.1.call-done = bf16[4,384,768]{2,1,0:T(8,128)(2,1)} async-done(((bf16[4,96,768]{2,1,0:T(8,128)(2,1)}), bf16[4,384,768]{2,1,0:T(8,128)(2,1)}) %all-gather.25.cloned.1.call-update) | async-done | bytes 2359312 | tf_op jit(solution)/shard_map/while/body/eval_jaxpr/all_gather | solution.py:292
  891.8 55.3 %all-gather.29.cloned.1.call-done = bf16[4,768,768]{2,1,0:T(8,128)(2,1)} async-done(((bf16[4,192,768]{2,1,0:T(8,128)(2,1)}), bf16[4,768,768]{2,1,0:T(8,128)(2,1)}) %all-gather.29.cloned.1.call-update) | async-done | bytes 4718608 | tf_op jit(solution)/shard_map/while/body/eval_jaxpr/all_gather | solution.py:296
  958.4 8.9 all-reduce.12
  967.4 8.0 all-gather.14
  975.5 7.7 all-gather.15
  983.3 5.9 convert_reduce_fusion.10
  989.2 10.8 fusion.431
  1000.0 12.8 fusion.432
  1027.3 15.3 all-gather.31.cloned.1.call-done
  1060.6 10.7 all-gather.35.cloned.1.call-done
  1076.7 53.5 %all-gather.37.cloned.1.call-done = bf16[2,768,1536]{2,1,0:T(8,128)(2,1)} async-done(((bf16[2,192,1536]{2,1,0:T(8,128)(2,1)}), bf16[2,768,1536]{2,1,0:T(8,128)(2,1)}) %all-gather.37.cloned.1.call-update) | async-done | bytes 4718608 | tf_op jit(solution)/shard_map/while/body/eval_jaxpr/all_gather | solution.py:301
  1133.6 36.2 %all-gather.39.cloned.1.call-done = bf16[1536,768]{1,0:T(8,128)(2,1)} async-done(((bf16[384,768]{1,0:T(8,128)(2,1)}), bf16[1536,768]{1,0:T(8,128)(2,1)}) %all-gather.39.cloned.1.call-update) | async-done | bytes 2359312 | tf_op jit(solution)/shard_map/while/body/eval_jaxpr/all_gather | solution.py:302
  1194.7 6.0 copy.136
  1200.8 6.2 fusion.448
  1207.0 6.1 copy.137
  1213.8 4.4 fusion.456
  1219.1 14.6 fusion.465
  1266.4 45.0 %reduce-scatter.31.cloned.1.call-done = f32[3,64,768]{2,1,0:T(8,128)} async-done(((f32[3,512,768]{2,1,0:T(8,128)}), f32[3,64,768]{2,1,0:T(8,128)}) %reduce-scatter.31.cloned.1.call-update) | async-done | bytes 589840 | tf_op jit(solution)/shard_map/while/body/eval_jaxpr/reduce_scatter | solution.py:176
  1332.2 24.1 %fusion.463 = bf16[128]{0:T(256)(128)(2,1)S(1)} fusion(bf16[128,16,1]{0,1,2:T(8,128)(2,1)S(1)} %copy-done.89, f32[64,512]{1,0:T(8,128)S(1)} %copy-done.57, f32[64,512]{1,0:T(8,128)S(1)} %copy-done.51, bf16[2,64,512,128]{3,2,1,0:T(8,128)(2,1)} %get-tuple-element.946, s32[]{:T(128)S(6)} %copy.165, f32[16,64,512]{2,1,0:T(8,128)} %get-tuple-element.831), kind=kOutput, calls=%fused_computation.10.clone.1 | convolution fusion | flops 826277760 | bytes 10752260 | tf_op jit(solution)/shard_map/while/body/eval_jaxpr/hij,ch->ijc/dot_general | solution.py:191
  1356.3 9.9 all-reduce.13
  1369.0 25.7 %reduce-scatter.39.cloned.1.call-done = bf16[2,96,768]{2,1,0:T(8,128)(2,1)} async-done(((bf16[2,384,768]{2,1,0:T(8,128)(2,1)}), bf16[2,96,768]{2,1,0:T(8,128)(2,1)}) %reduce-scatter.39.cloned.1.call-update) | async-done | bytes 294928 | tf_op jit(solution)/shard_map/while/body/eval_jaxpr/reduce_scatter | solution.py:325
  1396.7 29.5 %reduce-scatter.45.cloned.1.call-done = bf16[192,768]{1,0:T(8,128)(2,1)} async-done(((bf16[768,768]{1,0:T(8,128)(2,1)}), bf16[192,768]{1,0:T(8,128)(2,1)}) %reduce-scatter.45.cloned.1.call-update) | async-done | bytes 294928 | tf_op jit(solution)/shard_map/while/body/eval_jaxpr/reduce_scatter | solution.py:337
  1428.2 38.5 %reduce-scatter.51.cloned.1.call-done = bf16[384,768]{1,0:T(8,128)(2,1)} async-done(((bf16[1536,768]{1,0:T(8,128)(2,1)}), bf16[384,768]{1,0:T(8,128)(2,1)}) %reduce-scatter.51.cloned.1.call-update) | async-done | bytes 589840 | tf_op jit(solution)/shard_map/while/body/eval_jaxpr/reduce_scatter | solution.py:349
  1471.0 55.5 %reduce-scatter.49.cloned.1.call-done = bf16[2,192,1536]{2,1,0:T(8,128)(2,1)} async-done(((bf16[2,768,1536]{2,1,0:T(8,128)(2,1)}), bf16[2,192,1536]{2,1,0:T(8,128)(2,1)}) %reduce-scatter.49.cloned.1.call-update) | async-done | bytes 1179664 | tf_op jit(solution)/shard_map/while/body/eval_jaxpr/reduce_scatter | solution.py:346
  1530.5 22.5 %reduce-scatter.33.cloned.1.call-done = bf16[96,2]{1,0:T(8,128)(2,1)} async-done(((bf16[384,2]{1,0:T(8,128)(2,1)}), bf16[96,2]{1,0:T(8,128)(2,1)}) %reduce-scatter.33.cloned.1.call-update) | async-done | bytes 400 | tf_op jit(solution)/shard_map/while
  1553.8 26.1 %reduce-scatter.37.cloned.1.call-done = bf16[192,2]{1,0:T(8,128)(2,1)} async-done(((bf16[768,2]{1,0:T(8,128)(2,1)}), bf16[192,2]{1,0:T(8,128)(2,1)}) %reduce-scatter.37.cloned.1.call-update) | async-done | bytes 784 | tf_op jit(solution)/shard_map/while
  1580.9 39.7 %reduce-scatter.35.cloned.1.call-done = bf16[4,96,768]{2,1,0:T(8,128)(2,1)} async-done(((bf16[4,384,768]{2,1,0:T(8,128)(2,1)}), bf16[4,96,768]{2,1,0:T(8,128)(2,1)}) %reduce-scatter.35.cloned.1.call-update) | async-done | bytes 589840 | tf_op jit(solution)/shard_map/while/body/eval_jaxpr/reduce_scatter | solution.py:319
  1622.0 59.0 %reduce-scatter.43.cloned.1.call-done = bf16[4,192,768]{2,1,0:T(8,128)(2,1)} async-done(((bf16[4,768,768]{2,1,0:T(8,128)(2,1)}), bf16[4,192,768]{2,1,0:T(8,128)(2,1)}) %reduce-scatter.43.cloned.1.call-update) | async-done | bytes 1179664 | tf_op jit(solution)/shard_map/while/body/eval_jaxpr/reduce_scatter | solution.py:331
  1696.8 17.5 all-reduce.8
  1717.7 75.7 %all-reduce.16.cloned.1.call-done = (bf16[4,96,768]{2,1,0:T(8,128)(2,1)}, bf16[2,96,768]{2,1,0:T(8,128)(2,1)}, bf16[4,192,768]{2,1,0:T(8,128)(2,1)}, bf16[192,76...) async-done(((bf16[4,96,768]{2,1,0:T(8,128)(2,1)}, bf16[2,96,768]{2,1,0:T(8,128)(2,1)}, bf16[4,192,768]{2,1,0:T(8,128)(2,1)}, ...) | async-done | bytes 4128784 | tf_op jit(solution)/shard_map/psum | solution.py:361
  (883 shorter events, 334.3 us)
Async XLA Ops:
  8.4 43.1 %all-gather.25.cloned.1.call-start = ((), (), s32[]{:S(2)}) async-start(), calls=%async_computation.13 | async-start | bytes 2949120 | tf_op jit(solution)/shard_map/while/body/eval_jaxpr/all_gather | solution.py:292
  9.2 101.4 %all-gather.29.cloned.1.call-start = ((), (), s32[]{:S(2)}) async-start(), calls=%async_computation.15 | async-start | bytes 5898240 | tf_op jit(solution)/shard_map/while/body/eval_jaxpr/all_gather | solution.py:296
  9.9 169.7 %all-gather.27.cloned.1.call-start = ((), (), s32[]{:S(2)}) async-start(), calls=%async_computation.14 | async-start | bytes 1474560 | tf_op jit(solution)/shard_map/while/body/eval_jaxpr/all_gather | solution.py:294
  10.7 177.0 %all-gather.33.cloned.1.call-start = ((), (), s32[]{:S(2)}) async-start(), calls=%async_computation.17 | async-start | bytes 2654208 | tf_op jit(solution)/shard_map/while/body/eval_jaxpr/all_gather | solution.py:80
  29.4 153.9 %copy-start.20 = (bf16[1,3,64,384]{3,2,1,0:T(8,128)(2,1)}, bf16[1,3,64,384]{3,2,1,0:T(8,128)(2,1)S(1)}, u32[]{:S(2)}) copy-start(bf16[1,3,64,384]{3,2,1,0:T(8,128)(2,1)S(1)} %get-tuple-element.789) | copy-start | bytes 442372 | tf_op jit(solution)/shard_map/while
  29.4 208.6 %copy-start.71 = (f32[3,64]{1,0:T(4,128)}, f32[3,64]{1,0:T(4,128)S(1)}, u32[]{:S(2)}) copy-start(f32[3,64]{1,0:T(4,128)S(1)} %broadcast_multiply_fusion.10) | copy-start | bytes 2308 | tf_op jit(solution)/shard_map/while
  29.4 153.8 %copy-start.81 = (f32[384]{0:T(512)}, f32[384]{0:T(512)S(1)}, u32[]{:S(2)}) copy-start(f32[384]{0:T(512)S(1)} %get-tuple-element.790) | copy-start | bytes 4612 | tf_op jit(solution)/shard_map/while
  30.0 153.2 %copy-start.84 = (f32[3,64]{1,0:T(4,128)}, f32[3,64]{1,0:T(4,128)S(1)}, u32[]{:S(2)}) copy-start(f32[3,64]{1,0:T(4,128)S(1)} %add_rsqrt_fusion.4) | copy-start | bytes 2308 | tf_op jit(solution)/shard_map/while
  113.0 92.9 %all-gather.31.cloned.1.call-start = ((), (), s32[]{:S(2)}) async-start(), calls=%async_computation.16 | async-start | bytes 2654208 | tf_op jit(solution)/shard_map/while/body/eval_jaxpr/all_gather | solution.py:81
  115.5 119.2 %all-gather.35.cloned.1.call-start = ((), (), s32[]{:S(2)}) async-start(), calls=%async_computation.18 | async-start | bytes 1474560 | tf_op jit(solution)/shard_map/while/body/eval_jaxpr/all_gather | solution.py:298
  116.1 177.7 %all-gather.37.cloned.1.call-start = ((), (), s32[]{:S(2)}) async-start(), calls=%async_computation.19 | async-start | bytes 5898240 | tf_op jit(solution)/shard_map/while/body/eval_jaxpr/all_gather | solution.py:301
  116.8 216.4 %all-gather.39.cloned.1.call-start = ((), (), s32[]{:S(2)}) async-start(), calls=%async_computation.20 | async-start | bytes 2949120 | tf_op jit(solution)/shard_map/while/body/eval_jaxpr/all_gather | solution.py:302
  117.6 310.2 %reduce-scatter.29.cloned.1.call-start = ((), (), s32[]{:S(2)}) async-start(), calls=%async_computation.21 | async-start | bytes 5308416 | tf_op jit(solution)/shard_map/while/body/eval_jaxpr/reduce_scatter | solution.py:175
  119.6 224.3 %copy-start.67 = (f32[64]{0:T(128)}, f32[64]{0:T(128)S(1)}, u32[]{:S(2)}) copy-start(f32[64]{0:T(128)S(1)} %get-tuple-element.793) | copy-start | bytes 772 | tf_op jit(solution)/shard_map/while
  237.8 105.8 %copy-start.4 = (f32[3,64,768]{2,1,0:T(8,128)}, f32[3,64,768]{2,1,0:T(8,128)S(1)}, u32[]{:S(2)}) copy-start(f32[3,64,768]{2,1,0:T(8,128)S(1)} %get-tuple-element.804) | copy-start | bytes 1769476 | tf_op jit(solution)/shard_map/while
  240.0 95.9 %copy-start.52 = (bf16[3,64,768]{2,1,0:T(8,128)(2,1)}, bf16[3,64,768]{2,1,0:T(8,128)(2,1)S(1)}, u32[]{:S(2)}) copy-start(bf16[3,64,768]{2,1,0:T(8,128)(2,1)S(1)} %fusion.439) | copy-start | bytes 884740 | tf_op jit(solution)/shard_map/while
  364.2 110.7 %reduce-scatter.31.cloned.1.call-start = ((), (), s32[]{:S(2)}) async-start(), calls=%async_computation.22 | async-start | bytes 5308416 | tf_op jit(solution)/shard_map/while/body/eval_jaxpr/reduce_scatter | solution.py:176
  376.6 154.1 %reduce-scatter.41.cloned.1.call-start = ((), (), s32[]{:S(2)}) async-start(), calls=%async_computation.27 | async-start | bytes 245760 | tf_op jit(solution)/shard_map/while
  397.2 134.5 %reduce-scatter.47.cloned.1.call-start = ((), (), s32[]{:S(2)}) async-start(), calls=%async_computation.30 | async-start | bytes 40960 | tf_op jit(solution)/shard_map/while
  403.0 155.2 %reduce-scatter.39.cloned.1.call-start = ((), (), s32[]{:S(2)}) async-start(), calls=%async_computation.26 | async-start | bytes 1474560 | tf_op jit(solution)/shard_map/while/body/eval_jaxpr/reduce_scatter | solution.py:325
  405.5 184.1 %reduce-scatter.45.cloned.1.call-start = ((), (), s32[]{:S(2)}) async-start(), calls=%async_computation.29 | async-start | bytes 1474560 | tf_op jit(solution)/shard_map/while/body/eval_jaxpr/reduce_scatter | solution.py:337
  408.2 221.6 %reduce-scatter.51.cloned.1.call-start = ((), (), s32[]{:S(2)}) async-start(), calls=%async_computation.32 | async-start | bytes 2949120 | tf_op jit(solution)/shard_map/while/body/eval_jaxpr/reduce_scatter | solution.py:349
  411.7 278.1 %reduce-scatter.49.cloned.1.call-start = ((), (), s32[]{:S(2)}) async-start(), calls=%async_computation.31 | async-start | bytes 5898240 | tf_op jit(solution)/shard_map/while/body/eval_jaxpr/reduce_scatter | solution.py:346
  417.3 298.9 %reduce-scatter.33.cloned.1.call-start = ((), (), s32[]{:S(2)}) async-start(), calls=%async_computation.23 | async-start | bytes 122880 | tf_op jit(solution)/shard_map/while
  483.3 259.8 %reduce-scatter.37.cloned.1.call-start = ((), (), s32[]{:S(2)}) async-start(), calls=%async_computation.25 | async-start | bytes 245760 | tf_op jit(solution)/shard_map/while
  484.2 299.6 %reduce-scatter.35.cloned.1.call-start = ((), (), s32[]{:S(2)}) async-start(), calls=%async_computation.24 | async-start | bytes 2949120 | tf_op jit(solution)/shard_map/while/body/eval_jaxpr/reduce_scatter | solution.py:319
  487.5 356.5 %reduce-scatter.43.cloned.1.call-start = ((), (), s32[]{:S(2)}) async-start(), calls=%async_computation.28 | async-start | bytes 5898240 | tf_op jit(solution)/shard_map/while/body/eval_jaxpr/reduce_scatter | solution.py:331
  531.7 100.5 %copy-start.91 = (f32[2,192]{1,0:T(2,128)}, f32[2,192]{1,0:T(2,128)S(1)}, u32[]{:S(2)}) copy-start(f32[2,192]{1,0:T(2,128)S(1)} %select_add_fusion.26) | copy-start | bytes 4612 | tf_op jit(solution)/shard_map/while
  532.5 99.7 %copy-start.79 = (f32[32,16]{0,1:T(8,128)}, f32[32,16]{0,1:T(8,128)S(1)}, u32[]{:S(2)}) copy-start(f32[32,16]{0,1:T(8,128)S(1)} %select_add_fusion.30) | copy-start | bytes 6148 | tf_op jit(solution)/shard_map/while
  693.0 151.1 %copy-start.24 = (f32[4,192,768]{2,1,0:T(8,128)S(1)}, f32[4,192,768]{2,1,0:T(8,128)}, u32[]{:S(2)}) copy-start(f32[4,192,768]{2,1,0:T(8,128)} %get-tuple-element.885) | copy-start | bytes 7077892 | tf_op jit(solution)/shard_map/while
  717.1 129.0 %copy-start.105 = (f32[2,96]{1,0:T(2,128)}, f32[2,96]{1,0:T(2,128)S(1)}, u32[]{:S(2)}) copy-start(f32[2,96]{1,0:T(2,128)S(1)} %select_add_fusion.22) | copy-start | bytes 2308 | tf_op jit(solution)/shard_map/while
  744.0 102.1 %copy-start.94 = (f32[2,192]{1,0:T(2,128)}, f32[2,192]{1,0:T(2,128)S(1)}, u32[]{:S(2)}) copy-start(f32[2,192]{1,0:T(2,128)S(1)} %select_add_fusion.24) | copy-start | bytes 4612 | tf_op jit(solution)/shard_map/while
  847.7 40.3 %all-gather.25.cloned.1.call-start = ((), (), s32[]{:S(2)}) async-start(), calls=%async_computation.13 | async-start | bytes 2949120 | tf_op jit(solution)/shard_map/while/body/eval_jaxpr/all_gather | solution.py:292
  848.4 98.7 %all-gather.29.cloned.1.call-start = ((), (), s32[]{:S(2)}) async-start(), calls=%async_computation.15 | async-start | bytes 5898240 | tf_op jit(solution)/shard_map/while/body/eval_jaxpr/all_gather | solution.py:296
  849.2 167.0 %all-gather.27.cloned.1.call-start = ((), (), s32[]{:S(2)}) async-start(), calls=%async_computation.14 | async-start | bytes 1474560 | tf_op jit(solution)/shard_map/while/body/eval_jaxpr/all_gather | solution.py:294
  849.9 174.3 %all-gather.33.cloned.1.call-start = ((), (), s32[]{:S(2)}) async-start(), calls=%async_computation.17 | async-start | bytes 2654208 | tf_op jit(solution)/shard_map/while/body/eval_jaxpr/all_gather | solution.py:80
  866.2 153.6 %copy-start.20 = (bf16[1,3,64,384]{3,2,1,0:T(8,128)(2,1)}, bf16[1,3,64,384]{3,2,1,0:T(8,128)(2,1)S(1)}, u32[]{:S(2)}) copy-start(bf16[1,3,64,384]{3,2,1,0:T(8,128)(2,1)S(1)} %get-tuple-element.789) | copy-start | bytes 442372 | tf_op jit(solution)/shard_map/while
  866.2 208.4 %copy-start.71 = (f32[3,64]{1,0:T(4,128)}, f32[3,64]{1,0:T(4,128)S(1)}, u32[]{:S(2)}) copy-start(f32[3,64]{1,0:T(4,128)S(1)} %broadcast_multiply_fusion.10) | copy-start | bytes 2308 | tf_op jit(solution)/shard_map/while
  866.3 153.5 %copy-start.81 = (f32[384]{0:T(512)}, f32[384]{0:T(512)S(1)}, u32[]{:S(2)}) copy-start(f32[384]{0:T(512)S(1)} %get-tuple-element.790) | copy-start | bytes 4612 | tf_op jit(solution)/shard_map/while
  866.9 152.9 %copy-start.84 = (f32[3,64]{1,0:T(4,128)}, f32[3,64]{1,0:T(4,128)S(1)}, u32[]{:S(2)}) copy-start(f32[3,64]{1,0:T(4,128)S(1)} %add_rsqrt_fusion.4) | copy-start | bytes 2308 | tf_op jit(solution)/shard_map/while
  949.6 93.0 %all-gather.31.cloned.1.call-start = ((), (), s32[]{:S(2)}) async-start(), calls=%async_computation.16 | async-start | bytes 2654208 | tf_op jit(solution)/shard_map/while/body/eval_jaxpr/all_gather | solution.py:81
  952.1 119.3 %all-gather.35.cloned.1.call-start = ((), (), s32[]{:S(2)}) async-start(), calls=%async_computation.18 | async-start | bytes 1474560 | tf_op jit(solution)/shard_map/while/body/eval_jaxpr/all_gather | solution.py:298
  952.7 177.6 %all-gather.37.cloned.1.call-start = ((), (), s32[]{:S(2)}) async-start(), calls=%async_computation.19 | async-start | bytes 5898240 | tf_op jit(solution)/shard_map/while/body/eval_jaxpr/all_gather | solution.py:301
  953.2 216.5 %all-gather.39.cloned.1.call-start = ((), (), s32[]{:S(2)}) async-start(), calls=%async_computation.20 | async-start | bytes 2949120 | tf_op jit(solution)/shard_map/while/body/eval_jaxpr/all_gather | solution.py:302
  954.0 310.3 %reduce-scatter.29.cloned.1.call-start = ((), (), s32[]{:S(2)}) async-start(), calls=%async_computation.21 | async-start | bytes 5308416 | tf_op jit(solution)/shard_map/while/body/eval_jaxpr/reduce_scatter | solution.py:175
  956.0 224.4 %copy-start.67 = (f32[64]{0:T(128)}, f32[64]{0:T(128)S(1)}, u32[]{:S(2)}) copy-start(f32[64]{0:T(128)S(1)} %get-tuple-element.793) | copy-start | bytes 772 | tf_op jit(solution)/shard_map/while
  1074.4 105.7 %copy-start.4 = (f32[3,64,768]{2,1,0:T(8,128)}, f32[3,64,768]{2,1,0:T(8,128)S(1)}, u32[]{:S(2)}) copy-start(f32[3,64,768]{2,1,0:T(8,128)S(1)} %get-tuple-element.804) | copy-start | bytes 1769476 | tf_op jit(solution)/shard_map/while
  1200.8 110.7 %reduce-scatter.31.cloned.1.call-start = ((), (), s32[]{:S(2)}) async-start(), calls=%async_computation.22 | async-start | bytes 5308416 | tf_op jit(solution)/shard_map/while/body/eval_jaxpr/reduce_scatter | solution.py:176
  1213.2 154.1 %reduce-scatter.41.cloned.1.call-start = ((), (), s32[]{:S(2)}) async-start(), calls=%async_computation.27 | async-start | bytes 245760 | tf_op jit(solution)/shard_map/while
  1233.7 134.5 %reduce-scatter.47.cloned.1.call-start = ((), (), s32[]{:S(2)}) async-start(), calls=%async_computation.30 | async-start | bytes 40960 | tf_op jit(solution)/shard_map/while
  1239.5 155.2 %reduce-scatter.39.cloned.1.call-start = ((), (), s32[]{:S(2)}) async-start(), calls=%async_computation.26 | async-start | bytes 1474560 | tf_op jit(solution)/shard_map/while/body/eval_jaxpr/reduce_scatter | solution.py:325
  1242.0 184.2 %reduce-scatter.45.cloned.1.call-start = ((), (), s32[]{:S(2)}) async-start(), calls=%async_computation.29 | async-start | bytes 1474560 | tf_op jit(solution)/shard_map/while/body/eval_jaxpr/reduce_scatter | solution.py:337
  1244.8 221.9 %reduce-scatter.51.cloned.1.call-start = ((), (), s32[]{:S(2)}) async-start(), calls=%async_computation.32 | async-start | bytes 2949120 | tf_op jit(solution)/shard_map/while/body/eval_jaxpr/reduce_scatter | solution.py:349
  1248.3 278.3 %reduce-scatter.49.cloned.1.call-start = ((), (), s32[]{:S(2)}) async-start(), calls=%async_computation.31 | async-start | bytes 5898240 | tf_op jit(solution)/shard_map/while/body/eval_jaxpr/reduce_scatter | solution.py:346
  1253.9 299.1 %reduce-scatter.33.cloned.1.call-start = ((), (), s32[]{:S(2)}) async-start(), calls=%async_computation.23 | async-start | bytes 122880 | tf_op jit(solution)/shard_map/while
  1319.8 260.2 %reduce-scatter.37.cloned.1.call-start = ((), (), s32[]{:S(2)}) async-start(), calls=%async_computation.25 | async-start | bytes 245760 | tf_op jit(solution)/shard_map/while
  1320.7 299.8 %reduce-scatter.35.cloned.1.call-start = ((), (), s32[]{:S(2)}) async-start(), calls=%async_computation.24 | async-start | bytes 2949120 | tf_op jit(solution)/shard_map/while/body/eval_jaxpr/reduce_scatter | solution.py:319
  1324.0 357.0 %reduce-scatter.43.cloned.1.call-start = ((), (), s32[]{:S(2)}) async-start(), calls=%async_computation.28 | async-start | bytes 5898240 | tf_op jit(solution)/shard_map/while/body/eval_jaxpr/reduce_scatter | solution.py:331
  1368.2 101.1 %copy-start.91 = (f32[2,192]{1,0:T(2,128)}, f32[2,192]{1,0:T(2,128)S(1)}, u32[]{:S(2)}) copy-start(f32[2,192]{1,0:T(2,128)S(1)} %select_add_fusion.26) | copy-start | bytes 4612 | tf_op jit(solution)/shard_map/while
  1369.0 100.3 %copy-start.79 = (f32[32,16]{0,1:T(8,128)}, f32[32,16]{0,1:T(8,128)S(1)}, u32[]{:S(2)}) copy-start(f32[32,16]{0,1:T(8,128)S(1)} %select_add_fusion.30) | copy-start | bytes 6148 | tf_op jit(solution)/shard_map/while
  1530.5 150.5 %copy-start.24 = (f32[4,192,768]{2,1,0:T(8,128)S(1)}, f32[4,192,768]{2,1,0:T(8,128)}, u32[]{:S(2)}) copy-start(f32[4,192,768]{2,1,0:T(8,128)} %get-tuple-element.885) | copy-start | bytes 7077892 | tf_op jit(solution)/shard_map/while
  1553.8 129.1 %copy-start.105 = (f32[2,96]{1,0:T(2,128)}, f32[2,96]{1,0:T(2,128)S(1)}, u32[]{:S(2)}) copy-start(f32[2,96]{1,0:T(2,128)S(1)} %select_add_fusion.22) | copy-start | bytes 2308 | tf_op jit(solution)/shard_map/while
  1580.9 102.1 %copy-start.94 = (f32[2,192]{1,0:T(2,128)}, f32[2,192]{1,0:T(2,128)S(1)}, u32[]{:S(2)}) copy-start(f32[2,192]{1,0:T(2,128)S(1)} %select_add_fusion.24) | copy-start | bytes 4612 | tf_op jit(solution)/shard_map/while
  1686.7 106.6 %all-reduce.16.cloned.1.call-start = ((), (), s32[]{:S(2)}) async-start(), calls=%async_computation.12 | async-start | bytes 8257536 | tf_op jit(solution)/shard_map/psum | solution.py:361
  (218 other events, 3360.3 us)
Sparse Core Ops, SparseCore 0:
  11.3 40.1 all-gather.24
  53.5 57.0 all-gather.28
  112.6 27.8 all-gather.26
  142.0 31.6 all-gather.32
  175.2 30.7 all-gather.30
  207.8 26.8 all-gather.34
  236.6 57.0 all-gather.36
  295.7 37.4 all-gather.38
  364.4 54.9 reduce-scatter.28
  421.6 53.3 reduce-scatter.30
  477.9 22.3 reduce-scatter.40
  503.1 23.5 reduce-scatter.46
  529.6 28.5 reduce-scatter.38
  561.0 28.5 reduce-scatter.44
  592.4 37.3 reduce-scatter.50
  632.7 57.0 reduce-scatter.48
  692.4 23.7 reduce-scatter.32
  719.0 23.9 reduce-scatter.36
  746.4 37.3 reduce-scatter.34
  786.9 57.0 reduce-scatter.42
  850.5 37.4 all-gather.24
  890.0 57.0 all-gather.28
  949.1 27.7 all-gather.26
  978.5 31.6 all-gather.32
  1011.8 30.7 all-gather.30
  1044.5 26.8 all-gather.34
  1073.2 57.0 all-gather.36
  1132.3 37.4 all-gather.38
  1200.9 54.9 reduce-scatter.28
  1258.1 53.2 reduce-scatter.30
  1314.4 22.3 reduce-scatter.40
  1339.8 23.4 reduce-scatter.46
  1366.1 28.5 reduce-scatter.38
  1397.6 28.5 reduce-scatter.44
  1429.2 37.3 reduce-scatter.50
  1469.5 57.0 reduce-scatter.48
  1529.2 23.7 reduce-scatter.32
  1556.0 23.9 reduce-scatter.36
  1583.2 37.3 reduce-scatter.34
  1623.8 57.0 reduce-scatter.42
Sparse Core Ops, SparseCore 1:
  1696.1 97.2 all-reduce.15
where the time goes:
time: 1820 us; the launch traced here: 1810 us
  waiting for transfers between devices  1150 us (63%)
  matrix products  294 us (16%)
  other arithmetic  127 us (7%)
  blocking collectives  119 us (7%)
  local copies, waits for them, and re-layouts  88.3 us (5%)
    reduce_scatter x2, waiting for transfers between devices, one_batch(): lax.psum_scatter(grads[5].astype(jnp.bfloat16), 'sample', scatter_dimensi...  118 us
    reduce_scatter x2, waiting for transfers between devices, one_batch(): lax.psum_scatter(grads[10].astype(jnp.bfloat16), 'sample', scatter_dimens...  111 us
    all_gather x2, waiting for transfers between devices, one_batch(): lax.all_gather(attn_weight, 'sample', axis=1, tiled=True)  111 us
    all_gather x2, waiting for transfers between devices, one_batch(): lax.all_gather(trans_in, 'sample', axis=1, tiled=True)  107 us
    while x48, waiting for transfers between devices  106 us
    reduce_scatter x2, waiting for transfers between devices, layer_pass(): lax.psum_scatter(grad_value, 'row', scatter_dimension=1, tiled=True)  90.1 us
    reduce_scatter x2, waiting for transfers between devices, one_batch(): lax.psum_scatter(grads[1].astype(jnp.bfloat16), 'sample', scatter_dimensi...  79.5 us
    reduce_scatter x2, waiting for transfers between devices, one_batch(): lax.psum_scatter(grads[11].astype(jnp.bfloat16), 'sample', scatter_dimens...  76.9 us
  transfers between devices with their start and end apart: 41, of which 31 were waited for; matrix products, arithmetic and copies ran while one was open for 23% of the time, Pallas kernels for 0%

commit v1 on v0

v1 whole, which is shorter than its diff:
```python
import functools

import jax
import jax.numpy as jnp
from jax import lax
from jax.experimental import pallas as pl
from jax.experimental.pallas import tpu as pltpu
from jax.sharding import PartitionSpec as P

EPSILON = 1e-05
MASKED = -1000000000.0
F32 = jnp.float32
BF16 = jnp.bfloat16
VMEM_LIMIT = 58 << 20


def center_rows(value):
    center = value - jnp.mean(value, axis=-1, keepdims=True)
    rstd = lax.rsqrt(jnp.mean(center * center, axis=-1, keepdims=True) + EPSILON)
    return center * rstd, rstd


def dot(left, right):
    return lax.dot_general(left, right, (((1,), (0,)), ((), ())), preferred_element_type=F32)


def dot_nt(left, right):
    return lax.dot_general(left, right, (((1,), (1,)), ((), ())), preferred_element_type=F32)


def dot_tn(left, right):
    return lax.dot_general(left, right, (((0,), (0,)), ((), ())), preferred_element_type=F32)


def params(**extra):
    return pltpu.CompilerParams(vmem_limit_bytes=VMEM_LIMIT, **extra)


def head_windows(heads, head_dim):
    windows, head = [], 0
    while head < heads:
        start = head * head_dim // 128 * 128
        start = min(start, heads * head_dim - 256)
        inside = []
        while head < heads and (head + 1) * head_dim <= start + 256:
            inside.append(head)
            head += 1
        windows.append((start, inside))
    return windows


def head_mask(start, head, head_dim):
    lane = lax.broadcasted_iota(jnp.int32, (1, 256), 1) + start
    return (lane >= head * head_dim) & (lane < (head + 1) * head_dim)


def stack_heads(rows, start, inside, head_dim):
    zero = jnp.zeros_like(rows)
    return jnp.concatenate(
        [jnp.where(head_mask(start, head, head_dim), rows, zero) for head in inside], axis=0
    )


def unstack_heads(stacked, start, inside, head_dim):
    rows = stacked.shape[0] // len(inside)
    total = None
    for place, head in enumerate(inside):
        piece = jnp.where(
            head_mask(start, head, head_dim), stacked[place * rows : (place + 1) * rows], 0.0
        )
        total = piece if total is None else total + piece
    return total


def join_windows(parts, width):
    tiles = [None] * (width // 128)
    for start, value in parts:
        for half in range(2):
            place = start // 128 + half
            piece = value[:, half * 128 : (half + 1) * 128]
            tiles[place] = piece if tiles[place] is None else tiles[place] + piece
    return jnp.concatenate(tiles, axis=1)


def pair_kernel(meta_ref, pair_ref, mask_ref, gain_ref, weight_ref, low_ref, bias_ref):
    complex_id, block = pl.program_id(0), pl.program_id(1)
    rows, length = pair_ref.shape[1], pair_ref.shape[2]
    count = meta_ref[1 + complex_id]
    gain = gain_ref[...]
    weight = weight_ref[...]
    lines = []
    for row in range(rows):
        normed, _ = center_rows(pair_ref[0, row].astype(F32))
        low = (normed * gain).astype(BF16)
        low_ref[0, row] = low
        lines.append(dot_nt(weight, low))
    bias = jnp.stack(lines, axis=1)
    own = meta_ref[0] + block * rows + lax.broadcasted_iota(jnp.int32, (rows, length), 0)
    key = lax.broadcasted_iota(jnp.int32, (rows, length), 1)
    allowed = (key < count) & ((mask_ref[0] == 1) | (own == key) | (own >= count))
    bias_ref[0] = jnp.where(allowed[None], bias, MASKED)


def pair_bias(meta, pair, pair_mask, gain, weight):
    complexes, rows, length, width = pair.shape
    heads = weight.shape[1]
    block = 8
    return pl.pallas_call(
        pair_kernel,
        grid_spec=pltpu.PrefetchScalarGridSpec(
            num_scalar_prefetch=1,
            grid=(complexes, rows // block),
            in_specs=[
                pl.BlockSpec((1, block, length, width), lambda c, b, m: (c, b, 0, 0)),
                pl.BlockSpec((1, block, length), lambda c, b, m: (c, b, 0)),
                pl.BlockSpec((1, width), lambda c, b, m: (0, 0)),
                pl.BlockSpec((heads, width), lambda c, b, m: (0, 0)),
            ],
            out_specs=[
                pl.BlockSpec((1, block, length, width), lambda c, b, m: (c, b, 0, 0)),
                pl.BlockSpec((1, heads, block, length), lambda c, b, m: (c, 0, b, 0)),
            ],
        ),
        out_shape=[
            jax.ShapeDtypeStruct(pair.shape, BF16),
            jax.ShapeDtypeStruct((complexes, heads, rows, length), F32),
        ],
        compiler_params=params(),
        name="pair_bias",
    )(meta, pair, pair_mask, gain.astype(F32).reshape(1, width), weight.T)


def pair_grad_kernel(dbias_ref, low_ref, out_ref):
    first = (pl.program_id(0) == 0) & (pl.program_id(1) == 0)

    @pl.when(first)
    def _():
        out_ref[...] = jnp.zeros_like(out_ref)

    total = out_ref[...]
    for row in range(low_ref.shape[1]):
        total = total + dot(dbias_ref[0, :, row, :].astype(BF16), low_ref[0, row])
    out_ref[...] = total


def pair_grad(dbias, pair_low):
    complexes, rows, length, width = pair_low.shape
    heads = dbias.shape[1]
    block = 8
    return pl.pallas_call(
        pair_grad_kernel,
        grid=(complexes, rows // block),
        in_specs=[
            pl.BlockSpec((1, heads, block, length), lambda c, b: (c, 0, b, 0)),
            pl.BlockSpec((1, block, length, width), lambda c, b: (c, b, 0, 0)),
        ],
        out_specs=pl.BlockSpec((heads, width), lambda c, b: (0, 0)),
        out_shape=jax.ShapeDtypeStruct((heads, width), F32),
        compiler_params=params(),
        name="pair_grad",
    )(dbias, pair_low)


def project_kernel(
    tok_ref, single_ref, gain_ref, ada_ref, bias_ref, attn_ref, qbias_ref,
    normed_ref, query_ref, keyval_ref, gate_ref, hold_ref,
):
    which = pl.program_id(0)

    @pl.when(which == 0)
    def _():
        cond, _ = center_rows(single_ref[...].astype(F32))
        cond = (cond * gain_ref[0:1].astype(F32)).astype(BF16)
        pre = dot(cond, ada_ref[0]) + bias_ref[0:1].astype(F32)
        shift = dot(cond, ada_ref[1])
        normed, _ = center_rows(tok_ref[...].astype(F32))
        normed_in = (jax.nn.sigmoid(pre) * normed + shift).astype(BF16)
        normed_ref[...] = normed_in
        hold_ref[...] = normed_in

    result = dot(hold_ref[...], attn_ref[0])

    @pl.when(which == 0)
    def _():
        query_ref[...] = (result + qbias_ref[...].astype(F32)).astype(BF16)

    @pl.when((which == 1) | (which == 2))
    def _():
        keyval_ref[0] = result.astype(BF16)

    @pl.when(which == 3)
    def _():
        gate_ref[...] = jax.nn.sigmoid(result)


def project(tok, single, gain, ada, ada_bias, attn, query_bias):
    rows, width = tok.shape
    cond = single.shape[1]
    whole = lambda shape: pl.BlockSpec(shape, lambda w: (0,) * len(shape))
    return pl.pallas_call(
        project_kernel,
        grid=(4,),
        in_specs=[
            whole((rows, width)),
            whole((rows, cond)),
            whole((2, cond)),
            pl.BlockSpec((2, cond, width), lambda w: (0, 0, 0)),
            whole((2, width)),
            pl.BlockSpec((1, width, width), lambda w: (w, 0, 0)),
            whole((1, width)),
        ],
        out_specs=[
            whole((rows, width)),
            whole((rows, width)),
            pl.BlockSpec((1, rows, width), lambda w: (jnp.clip(w - 1, 0, 1), 0, 0)),
            whole((rows, width)),
        ],
        out_shape=[
            jax.ShapeDtypeStruct((rows, width), BF16),
            jax.ShapeDtypeStruct((rows, width), BF16),
            jax.ShapeDtypeStruct((2, rows, width), BF16),
            jax.ShapeDtypeStruct((rows, width), F32),
        ],
        scratch_shapes=[pltpu.VMEM((rows, width), BF16)],
        compiler_params=params(),
        name="project",
    )(tok, single, gain, ada, ada_bias, attn, query_bias.reshape(1, width))


def attend_kernel(heads, query_ref, key_ref, value_ref, bias_ref, out_ref, prob_ref):
    rows, width = query_ref.shape[2], query_ref.shape[3]
    length = key_ref.shape[2]
    head_dim = width // heads
    scale = head_dim ** (-0.5)
    parts = []
    for start, inside in head_windows(heads, head_dim):
        count = len(inside)
        lanes = slice(start, start + 256)
        stacked = stack_heads(query_ref[0, 0, :, lanes], start, inside, head_dim)
        scores = dot_nt(stacked, key_ref[0, 0, :, lanes]) * scale
        bias = bias_ref[0, inside[0] : inside[-1] + 1].reshape(count * rows, length)
        scores = scores + bias
        weight = jnp.exp(scores - jnp.max(scores, axis=-1, keepdims=True))
        prob = weight * (1.0 / jnp.sum(weight, axis=-1, keepdims=True))
        low = prob.astype(BF16)
        prob_ref[0, 0, inside[0] : inside[-1] + 1] = low.reshape(count, rows, length)
        mixed = dot(low, value_ref[0, 0, :, lanes])
        parts.append((start, unstack_heads(mixed, start, inside, head_dim)))
    out_ref[0, 0] = join_windows(parts, width)


def attend(query, key, value, bias):
    complexes, samples, rows, width = query.shape
    heads, length = bias.shape[1], bias.shape[3]
    own = pl.BlockSpec((1, 1, rows, width), lambda c, s: (c, s, 0, 0))
    full = pl.BlockSpec((1, 1, length, width), lambda c, s: (c, s, 0, 0))
    return pl.pallas_call(
        functools.partial(attend_kernel, heads),
        grid=(complexes, samples),
        in_specs=[
            own,
            full,
            full,
            pl.BlockSpec((1, heads, rows, length), lambda c, s: (c, 0, 0, 0)),
        ],
        out_specs=[
            own,
            pl.BlockSpec((1, 1, heads, rows, length), lambda c, s: (c, s, 0, 0, 0)),
        ],
        out_shape=[
            jax.ShapeDtypeStruct((complexes, samples, rows, width), F32),
            jax.ShapeDtypeStruct((complexes, samples, heads, rows, length), BF16),
        ],
        compiler_params=params(),
        name="attend",
    )(query, key, value, bias)


def attend_back_kernel(
    heads, prob_ref, grad_ref, query_ref, key_ref, value_ref, dq_ref, dk_ref, dv_ref, dbias_ref
):
    rows, width = query_ref.shape[2], query_ref.shape[3]
    length = key_ref.shape[2]
    head_dim = width // heads
    scale = head_dim ** (-0.5)

    @pl.when(pl.program_id(1) == 0)
    def _():
        dbias_ref[...] = jnp.zeros_like(dbias_ref)

    dq_parts, dk_parts, dv_parts = [], [], []
    for start, inside in head_windows(heads, head_dim):
        count = len(inside)
        lanes = slice(start, start + 256)
        queries = stack_heads(query_ref[0, 0, :, lanes], start, inside, head_dim)
        grads = stack_heads(grad_ref[0, 0, :, lanes], start, inside, head_dim)
        span = slice(inside[0], inside[-1] + 1)
        low = prob_ref[0, 0, span].reshape(count * rows, length)
        prob = low.astype(F32)
        dprob = dot_nt(grads, value_ref[0, 0, :, lanes])
        inner = jnp.sum(prob * dprob, axis=-1, keepdims=True)
        dscore = (prob * (dprob - inner)).astype(BF16)
        dbias_ref[0, span] += dscore.astype(F32).reshape(count, rows, length)
        mixed = dot(dscore, key_ref[0, 0, :, lanes])
        dq_parts.append((start, unstack_heads(mixed, start, inside, head_dim)))
        dk_parts.append((start, dot_tn(dscore, queries)))
        dv_parts.append((start, dot_tn(low, grads)))
    dq_ref[0, 0] = (join_windows(dq_parts, width) * scale).astype(BF16)
    dk_ref[0, 0] = (join_windows(dk_parts, width) * scale).astype(BF16)
    dv_ref[0, 0] = join_windows(dv_parts, width).astype(BF16)


def attend_back(prob, grad, query, key, value):
    complexes, samples, rows, width = query.shape
    heads, length = prob.shape[2], prob.shape[4]
    own = pl.BlockSpec((1, 1, rows, width), lambda c, s: (c, s, 0, 0))
    full = pl.BlockSpec((1, 1, length, width), lambda c, s: (c, s, 0, 0))
    return pl.pallas_call(
        functools.partial(attend_back_kernel, heads),
        grid=(complexes, samples),
        in_specs=[
            pl.BlockSpec((1, 1, heads, rows, length), lambda c, s: (c, s, 0, 0, 0)),
            own,
            own,
            full,
            full,
        ],
        out_specs=[
            own,
            full,
            full,
            pl.BlockSpec((1, heads, rows, length), lambda c, s: (c, 0, 0, 0)),
        ],
        out_shape=[
            jax.ShapeDtypeStruct((complexes, samples, rows, width), BF16),
            jax.ShapeDtypeStruct((complexes, samples, length, width), BF16),
            jax.ShapeDtypeStruct((complexes, samples, length, width), BF16),
            jax.ShapeDtypeStruct((complexes, heads, rows, length), F32),
        ],
        compiler_params=params(),
        name="attend_back",
    )(prob, grad, query, key, value)


def middle_kernel(
    samples, rows_dev, meta_ref,
    att_ref, gate_ref, tok_ref, single_ref, cot_ref,
    gain_ref, ada_ref, ada_bias_ref, zero_ref, zero_bias_ref, out_w_ref, tin_ref, tout_ref,
    out_ref, dmid_ref, datt_ref, dglogit_ref,
    gated_ref, dabranch_ref, dza_ref, dzb_ref, tcond_ref, dtpre_ref, dtin_ref,
    tinput_ref, dfirst_ref, dsecond_ref, hidden_ref, dtbranch_ref, small_ref,
):
    step = pl.program_id(0)
    rows = att_ref.shape[0]
    count = meta_ref[1 + step]
    place = lax.broadcasted_iota(jnp.int32, (rows, 1), 0) % rows_dev + meta_ref[0]
    valid = (place < count).astype(F32)
    att = att_ref[...]
    gate = gate_ref[...]
    single = single_ref[...]
    gated = (att * gate).astype(BF16)
    gated_ref[...] = gated
    branch = dot(gated, out_w_ref[...])
    attn_zero = jax.nn.sigmoid(dot(single, zero_ref[0]) + zero_bias_ref[0:1].astype(F32))
    middle = tok_ref[...].astype(F32) + valid * attn_zero * branch
    cond, _ = center_rows(single.astype(F32))
    tcond = (cond * gain_ref[1:2].astype(F32)).astype(BF16)
    tcond_ref[...] = tcond
    scale = jax.nn.sigmoid(dot(tcond, ada_ref[0]) + ada_bias_ref[1:2].astype(F32))
    shift = dot(tcond, ada_ref[1])
    normed, rstd = center_rows(middle)
    tinput = (scale * normed + shift).astype(BF16)
    tinput_ref[...] = tinput
    first = dot(tinput, tin_ref[0])
    second = dot(tinput, tin_ref[1])
    sig = jax.nn.sigmoid(first)
    hidden = (first * sig * second).astype(BF16)
    hidden_ref[...] = hidden
    tbranch = dot(hidden, tout_ref[...])
    trans_zero = jax.nn.sigmoid(dot(single, zero_ref[1]) + zero_bias_ref[1:2].astype(F32))
    out_ref[...] = (middle + valid * trans_zero * tbranch).astype(BF16)
    grad_out = cot_ref[...].astype(F32)
    gated_out = grad_out * valid
    dtbranch = (gated_out * trans_zero).astype(BF16)
    dtbranch_ref[...] = dtbranch
    dzb = (gated_out * tbranch * trans_zero * (1.0 - trans_zero)).astype(BF16)
    dzb_ref[...] = dzb
    dhidden = dot_nt(dtbranch, tout_ref[...])
    dfirst = (dhidden * second * sig * (1.0 + first * (1.0 - sig))).astype(BF16)
    dsecond = (dhidden * first * sig).astype(BF16)
    dfirst_ref[...] = dfirst
    dsecond_ref[...] = dsecond
    dtin = (dot_nt(dfirst, tin_ref[0]) + dot_nt(dsecond, tin_ref[1])).astype(BF16)
    dtin_ref[...] = dtin
    dtin_full = dtin.astype(F32)
    dtpre = (dtin_full * normed * scale * (1.0 - scale)).astype(BF16)
    dtpre_ref[...] = dtpre
    grad_norm = dtin_full * scale
    tail = grad_norm - jnp.mean(grad_norm, axis=-1, keepdims=True)
    tail = tail - normed * jnp.mean(grad_norm * normed, axis=-1, keepdims=True)
    dmid = grad_out + tail * rstd
    dmid_ref[...] = dmid
    dtcond = dot_nt(dtpre, ada_ref[0]) + dot_nt(dtin, ada_ref[1])
    gated_mid = dmid * valid
    dabranch = (gated_mid * attn_zero).astype(BF16)
    dabranch_ref[...] = dabranch
    dza = (gated_mid * branch * attn_zero * (1.0 - attn_zero)).astype(BF16)
    dza_ref[...] = dza
    dgated = dot_nt(dabranch, out_w_ref[...])
    datt_ref[...] = (dgated * gate).astype(BF16)
    dglogit_ref[...] = (dgated * att * gate * (1.0 - gate)).astype(BF16)

    @pl.when(step == 0)
    def _():
        small_ref[...] = jnp.zeros_like(small_ref)

    width, narrow = att.shape[1], single.shape[1]
    total = lambda value: jnp.sum(value.astype(F32), axis=0, keepdims=True)
    small_ref[0:1, :] += total(dtpre)
    small_ref[1:2, :] += total(dza)
    small_ref[2:3, :] += total(dzb)
    small_ref[3:4, 0:narrow] += total(dtcond * cond)


def middle_pass(
    meta, att, gate, tok, single, cot, gain, ada, ada_bias, zero, zero_bias, out_w, trans_in,
    trans_out, complexes, samples, rows_dev,
):
    rows, width = tok.shape
    narrow = single.shape[1]
    hidden = trans_out.shape[0]
    part = rows // complexes
    wide = pl.BlockSpec((part, width), lambda c, m: (c, 0))
    slim = pl.BlockSpec((part, narrow), lambda c, m: (c, 0))
    long = pl.BlockSpec((part, hidden), lambda c, m: (c, 0))
    once = lambda shape: pl.BlockSpec(
        shape, lambda c, m: (0,) * len(shape), pipeline_mode=pl.Buffered(1)
    )
    shape = lambda cols, kind: jax.ShapeDtypeStruct((rows, cols), kind)
    return pl.pallas_call(
        functools.partial(middle_kernel, samples, rows_dev),
        grid_spec=pltpu.PrefetchScalarGridSpec(
            num_scalar_prefetch=1,
            grid=(complexes,),
            in_specs=[
                wide, wide, wide, slim, wide,
                once(gain.shape),
                pl.BlockSpec((2, narrow, width), lambda c, m: (1, 0, 0), pipeline_mode=pl.Buffered(1)),
                once(ada_bias.shape),
                once(zero.shape),
                once(zero_bias.shape),
                once(out_w.shape),
                once(trans_in.shape),
                once(trans_out.shape),
            ],
            out_specs=[
                wide, wide, wide, wide,
                wide, wide, wide, wide, slim, wide, wide,
                wide, long, long, long, wide,
                once((8, width)),
            ],
        ),
        out_shape=[
            shape(width, BF16), shape(width, F32), shape(width, BF16), shape(width, BF16),
            shape(width, BF16), shape(width, BF16), shape(width, BF16), shape(width, BF16),
            shape(narrow, BF16), shape(width, BF16), shape(width, BF16),
            shape(width, BF16), shape(hidden, BF16), shape(hidden, BF16), shape(hidden, BF16),
            shape(width, BF16),
            jax.ShapeDtypeStruct((8, width), F32),
        ],
        compiler_params=params(),
        name="middle_pass",
    )(meta, att, gate, tok, single, cot, gain, ada, ada_bias, zero, zero_bias, out_w, trans_in, trans_out)


def last_kernel(
    dquery_ref, dkey_ref, dvalue_ref, dglogit_ref, tok_ref, single_ref, dmid_ref,
    gain_ref, ada_ref, ada_bias_ref, attn_ref,
    tgrad_ref, dnormed_ref, dapre_ref, cond_ref, small_ref, acc_ref,
):
    which = pl.program_id(0)

    @pl.when(which == 0)
    def _():
        acc_ref[...] = dot_nt(dquery_ref[...], attn_ref[0])

    @pl.when(which == 1)
    def _():
        acc_ref[...] += dot_nt(dkey_ref[...], attn_ref[0])

    @pl.when(which == 2)
    def _():
        acc_ref[...] += dot_nt(dvalue_ref[...], attn_ref[0])

    @pl.when(which == 3)
    def _():
        dnormed = (acc_ref[...] + dot_nt(dglogit_ref[...], attn_ref[0])).astype(BF16)
        dnormed_ref[...] = dnormed
        cond, _ = center_rows(single_ref[...].astype(F32))
        cond_low = (cond * gain_ref[0:1].astype(F32)).astype(BF16)
        cond_ref[...] = cond_low
        scale = jax.nn.sigmoid(dot(cond_low, ada_ref[0]) + ada_bias_ref[0:1].astype(F32))
        normed, rstd = center_rows(tok_ref[...].astype(F32))
        full = dnormed.astype(F32)
        dapre = (full * normed * scale * (1.0 - scale)).astype(BF16)
        dapre_ref[...] = dapre
        grad_norm = full * scale
        tail = grad_norm - jnp.mean(grad_norm, axis=-1, keepdims=True)
        tail = tail - normed * jnp.mean(grad_norm * normed, axis=-1, keepdims=True)
        tgrad_ref[...] = dmid_ref[...] + tail * rstd
        dcond = dot_nt(dapre, ada_ref[0]) + dot_nt(dnormed, ada_ref[1])
        narrow = cond.shape[1]
        total = lambda value: jnp.sum(value.astype(F32), axis=0, keepdims=True)
        small_ref[...] = jnp.zeros_like(small_ref)
        small_ref[0:1, :] = total(dapre)
        small_ref[1:2, :] = total(dquery_ref[...])
        small_ref[2:3, 0:narrow] = total(dcond * cond)


def last_pass(dquery, dkey, dvalue, dglogit, tok, single, dmid, gain, ada, ada_bias, attn):
    rows, width = tok.shape
    narrow = single.shape[1]
    whole = lambda shape: pl.BlockSpec(shape, lambda w: (0,) * len(shape))
    wide = whole((rows, width))
    shape = lambda cols, kind: jax.ShapeDtypeStruct((rows, cols), kind)
    return pl.pallas_call(
        last_kernel,
        grid=(4,),
        in_specs=[
            wide, wide, wide, wide, wide, whole((rows, narrow)), wide,
            whole(gain.shape),
            pl.BlockSpec((2, narrow, width), lambda w: (0, 0, 0)),
            whole(ada_bias.shape),
            pl.BlockSpec((1, width, width), lambda w: (w, 0, 0)),
        ],
        out_specs=[wide, wide, wide, whole((rows, narrow)), whole((8, width))],
        out_shape=[
            shape(width, F32), shape(width, BF16), shape(width, BF16), shape(narrow, BF16),
            jax.ShapeDtypeStruct((8, width), F32),
        ],
        scratch_shapes=[pltpu.VMEM((rows, width), F32)],
        compiler_params=params(),
        name="last_pass",
    )(dquery, dkey, dvalue, dglogit, tok, single, dmid, gain, ada, ada_bias, attn)


def weight_grad(left, grads):
    return [dot_tn(left, grad).astype(BF16) for grad in grads]


def gather_weights(shards, axes):
    return [
        lax.all_gather(shard, "sample", axis=axis, tiled=True) for shard, axis in zip(shards, axes)
    ]


def local(
    tokens, single, pair, token_count, pair_mask, cotangent, cond_gain, ada_weight, ada_bias,
    zero_weight, zero_bias, attn_weight, query_bias, out_weight, pair_gain, pair_weight,
    trans_in, trans_out,
):
    complexes, samples, rows_dev, width = tokens.shape
    narrow = single.shape[3]
    heads = pair_weight.shape[1]
    length = pair.shape[2]
    own_start = (lax.axis_index("row") * rows_dev).astype(jnp.int32)
    meta = jnp.concatenate([own_start[None], token_count.astype(jnp.int32)])
    full = gather_weights(
        (cond_gain, ada_weight, ada_bias, zero_weight, zero_bias, attn_weight, query_bias,
         out_weight, pair_gain, pair_weight, trans_in, trans_out),
        (1, 1, 1, 1, 1, 1, 0, 0, 0, 0, 1, 0),
    )
    (gain, ada, ada_b, zero, zero_b, attn, query_b, out_w, pgain, pweight, tin, tout) = full
    rows = complexes * samples * rows_dev
    flat = lambda value: value.reshape(rows, value.shape[-1])
    block = lambda value: value.reshape(complexes, samples, rows_dev, width)
    tok, sing, cot = flat(tokens), flat(single), flat(cotangent)

    pair_low, bias = pair_bias(meta, pair, pair_mask, pgain, pweight)
    normed_in, query, keyval, gate = project(tok, sing, gain, ada, ada_b, attn, query_b)
    query = block(query)
    key_all = lax.all_gather(block(keyval[0]), "row", axis=2, tiled=True)
    value_all = lax.all_gather(block(keyval[1]), "row", axis=2, tiled=True)
    att, prob = attend(query, key_all, value_all, bias)
    (
        output, dmid, datt, dglogit, gated, dabranch, dza, dzb, tcond, dtpre, dtin, tinput,
        dfirst, dsecond, hidden, dtbranch, small_mid,
    ) = middle_pass(
        meta, flat(att), gate, tok, sing, cot, gain, ada, ada_b, zero, zero_b, out_w, tin, tout,
        complexes, samples, rows_dev,
    )
    dquery, dkey, dvalue, dbias = attend_back(prob, block(datt), query, key_all, value_all)
    dkey_own = lax.psum_scatter(dkey, "row", scatter_dimension=2, tiled=True)
    dvalue_own = lax.psum_scatter(dvalue, "row", scatter_dimension=2, tiled=True)
    pair_sum = pair_grad(dbias, pair_low)
    dquery, dkey_own, dvalue_own = flat(dquery), flat(dkey_own), flat(dvalue_own)
    tgrad, dnormed, dapre, cond, small_last = last_pass(
        dquery, dkey_own, dvalue_own, dglogit, tok, sing, dmid, gain, ada, ada_b, attn
    )
    ada_grad = jnp.stack(weight_grad(cond, [dapre, dnormed]) + weight_grad(tcond, [dtpre, dtin]))
    zero_grad = jnp.stack(weight_grad(sing, [dza, dzb]))
    attn_grad = jnp.stack(weight_grad(normed_in, [dquery, dkey_own, dvalue_own, dglogit]))
    out_grad = weight_grad(gated, [dabranch])[0]
    tin_grad = jnp.stack(weight_grad(tinput, [dfirst, dsecond]))
    tout_grad = weight_grad(hidden, [dtbranch])[0]

    def reduce(value, axis):
        part = lax.psum_scatter(value, "sample", scatter_dimension=axis, tiled=True)
        return lax.psum(part, "row").astype(F32)

    small = jnp.concatenate(
        [small_mid.reshape(-1), small_last.reshape(-1), pair_sum.reshape(-1)]
    )
    small = lax.psum(small, ("row", "sample"))
    mid_size = small_mid.size
    small_mid = small[:mid_size].reshape(small_mid.shape)
    small_last = small[mid_size : 2 * mid_size].reshape(small_last.shape)
    pair_sum = small[2 * mid_size :].reshape(pair_sum.shape)
    spot = lax.axis_index("sample")

    def own_part(value, axis):
        size = value.shape[axis] // lax.axis_size("sample")
        return lax.dynamic_slice_in_dim(value, spot * size, size, axis)

    gain_grad = own_part(jnp.stack([small_last[2, :narrow], small_mid[3, :narrow]]), 1)
    ada_bias_grad = own_part(jnp.stack([small_last[0], small_mid[0]]), 1)
    zero_bias_grad = own_part(small_mid[1:3], 1)
    query_bias_grad = own_part(small_last[1], 0)
    pair_gain_grad = own_part(
        jnp.sum(pweight.astype(F32).T * pair_sum, axis=0) / pgain.astype(F32), 0
    )
    pair_weight_grad = own_part(pair_sum.T, 0)
    return (
        output.reshape(tokens.shape),
        tgrad.reshape(tokens.shape),
        gain_grad,
        reduce(ada_grad, 1),
        ada_bias_grad,
        reduce(zero_grad, 1),
        zero_bias_grad,
        reduce(attn_grad, 1),
        query_bias_grad,
        reduce(out_grad, 0),
        pair_gain_grad,
        pair_weight_grad,
        reduce(tin_grad, 1),
        reduce(tout_grad, 0),
    )


def solution(mesh):
    rowwise = P(None, "sample", "row", None)
    return jax.shard_map(
        local,
        mesh=mesh,
        in_specs=(
            rowwise,
            rowwise,
            P(None, "row", None, None),
            P(),
            P(None, "row", None),
            rowwise,
            P(None, "sample"),
            P(None, "sample", None),
            P(None, "sample"),
            P(None, "sample", None),
            P(None, "sample"),
            P(None, "sample", None),
            P("sample"),
            P("sample", None),
            P("sample"),
            P("sample", None),
            P(None, "sample", None),
            P("sample", None),
        ),
        out_specs=(
            rowwise,
            rowwise,
            P(None, "sample"),
            P(None, "sample", None),
            P(None, "sample"),
            P(None, "sample", None),
            P(None, "sample"),
            P(None, "sample", None),
            P("sample"),
            P("sample", None),
            P("sample"),
            P("sample", None),
            P(None, "sample", None),
            P("sample", None),
        ),
        check_vma=False,
    )
```

time: 1820 us -> 942 us (0.52)
  waiting for transfers between devices: 1150 us -> 671 us
  matrix products: 294 us -> 15 us
  Pallas kernels: 0 us -> 114 us
  other arithmetic: 127 us -> 17.7 us
  local copies, waits for them, and re-layouts: 88.3 us -> 22.2 us
  blocking collectives: 119 us -> 83 us
    dot_general x98 -> x14, matrix products: 294 us -> 15 us  [dot_tn(): lax.dot_general(left, right, (((0,), (0,)), ((), ())), preferred_element_...]
    reduce_scatter x16 -> x7, waiting for transfers between devices: 586 us -> 322 us  [the longest x5 233 us: reduce(): part = lax.psum_scatter(value, 'sample', scatter_dimension=axis, tiled=True)]
    all_gather x16 -> x8, waiting for transfers between devices: 384 us -> 269 us  [the longest x6 213 us: gather_weights(): lax.all_gather(shard, 'sample', axis=axis, tiled=True)]
    pallas_call x0 -> x7, Pallas kernels: none -> 114 us  [the longest x1 27.3 us: pair_bias(): pl.pallas_call(pair_kernel, grid_spec=pltpu.PrefetchScalarGridSpec(num_sc...]
    while x48 -> x0, waiting for transfers between devices: 106 us -> none
    reduce_sum x26 -> x1, other arithmetic: 48.2 us -> 0.02 us  [local(): jnp.sum(pweight.astype(F32).T * pair_sum, axis=0) / pgain.astype(F32)]
    unnamed x1 -> x18, waiting for transfers between devices: 0.02 us -> 39.6 us
    while x4 -> x0, blocking collectives: 37.5 us -> none
  transfers between devices with their start and end apart: 41 -> 17, of which waited for: 31 -> 17; matrix products, arithmetic and copies ran while one was open for 23% -> 4% of each run, Pallas kernels for 0% -> 7%
where the time goes in v1:
time: 942 us; the launch traced here: 940 us
  waiting for transfers between devices  671 us (71%)
  Pallas kernels  114 us (12%)
  blocking collectives  83 us (9%)
  local copies, waits for them, and re-layouts  22.2 us (2%)
  other arithmetic  17.7 us (2%)
  between operations  16.4 us (2%)
  matrix products  15 us (2%)
    reduce_scatter x5, waiting for transfers between devices, reduce(): part = lax.psum_scatter(value, 'sample', scatter_dimension=axis, tiled=True)  233 us
    all_gather x6, waiting for transfers between devices, gather_weights(): lax.all_gather(shard, 'sample', axis=axis, tiled=True)  213 us
    reduce_scatter x1, waiting for transfers between devices, local(): lax.psum_scatter(dvalue, 'row', scatter_dimension=2, tiled=True)  55.5 us
    all_gather x1, waiting for transfers between devices, local(): value_all = lax.all_gather(block(keyval[1]), 'row', axis=2, tiled=True)  52.6 us
    psum x1, blocking collectives, local(): small = lax.psum(small, ('row', 'sample'))  41.3 us
    psum x1, waiting for transfers between devices, reduce(): return lax.psum(part, 'row').astype(F32)  40.1 us
    unnamed x18, waiting for transfers between devices  39.6 us
    reduce_scatter x1, waiting for transfers between devices, local(): dkey_own = lax.psum_scatter(dkey, 'row', scatter_dimension=2, tiled=True)  33.4 us
  transfers between devices with their start and end apart: 17, of which 17 were waited for; matrix products, arithmetic and copies ran while one was open for 4% of the time, Pallas kernels for 7%

profile of v1, /device:TPU:0, one launch (start us, length us, event | category | flops | bytes accessed | tf_op | source)
XLA Modules:
  0.0 940.4 jit_solution(11122273243030423)
XLA Ops:
  7.3 0.7 all-gather.13.cloned.1.call-update
  8.0 0.7 all-gather.15.cloned.1.call-update
  11.2 11.3 %all-reduce.4 = (bf16[768]{0:T(1024)(128)(2,1)S(1)}, bf16[128]{0:T(256)(128)(2,1)S(1)}) all-reduce(bf16[768]{0:T(1024)(128)(2,1)S(1)} %dynamic-update-slice, bf16[128]{0:T(256)(128)(2,1)S(1)} %dynamic-update-slice.1), channel_id=1, replica_groups=mesh['row'=8,'sample'=4] {'sample'}, use_global_device_ids=true, to_apply=%add | all-reduce | flops 896 | bytes 3584
  23.1 7.1 all-gather.1
  30.9 7.9 all-gather
  39.4 10.8 %all-gather.13.cloned.1.call-done.ada_ref = bf16[4,384,768]{2,1,0:T(8,128)(2,1)} async-done(((bf16[4,96,768]{2,1,0:T(8,128)(2,1)}), bf16[4,384,768]{2,1,0:T(8,128)(2,1)}) %all-gather.13.cloned.1.call-update) | async-done | bytes 2359312 | tf_op jit(solution)/shard_map/all_gather | solution.py:553
  50.2 58.9 %all-gather.15.cloned.1.call-done.attn_ref = bf16[4,768,768]{2,1,0:T(8,128)(2,1)} async-done(((bf16[4,192,768]{2,1,0:T(8,128)(2,1)}), bf16[4,768,768]{2,1,0:T(8,128)(2,1)}) %all-gather.15.cloned.1.call-update) | async-done | bytes 4718608 | tf_op jit(solution)/shard_map/all_gather | solution.py:553
  109.1 8.4 project.1
  117.5 2.3 fusion.14
  121.7 0.7 all-gather.27.cloned.1.call-update
  122.4 0.7 all-gather.25.cloned.1.call-update
  123.2 8.1 all-gather.2
  131.3 0.7 reshape.128
  132.0 7.3 all-gather.3
  139.3 0.7 reshape.130
  141.1 27.3 %pair_bias.1 = (bf16[2,64,512,128]{3,2,1,0:T(8,128)(2,1)}, f32[2,16,64,512]{3,2,1,0:T(8,128)}) custom-call(s32[3]{0:T(128)} %pad_add_fusion.meta_ref, bf16[2,64,512,128]{3,2,1,0:T(8,128)(2,1)} %pair_ref.1, s32[2,64,512]{2,1,0:T(8,128)} %mask_ref.1, f32[1,128]{1,0:T(1,128)} %convert_bitcast_fusion.gain_ref, bf16[16,128]{1,0:T(8,128)(2,1)} %bitcast.129), custom_call_target="tpu_custom_call" | custom-call | tf_op jit(solution)/shard_map/pair_bias/pallas_call | solution.py:108
  168.3 3.4 all-gather.17.cloned.1.call-done.key_ref
  171.7 52.6 %all-gather.19.cloned.1.call-done.value_ref = bf16[2,3,512,768]{3,2,1,0:T(8,128)(2,1)} async-done(((bf16[2,3,64,768]{3,2,1,0:T(8,128)(2,1)}), bf16[2,3,512,768]{3,2,1,0:T(8,128)(2,1)}) %all-gather.19.cloned.1.call-update) | async-done | bytes 4718608 | tf_op jit(solution)/shard_map/all_gather | solution.py:583
  224.3 12.9 %attend.1 = (f32[2,3,64,768]{3,2,1,0:T(8,128)}, bf16[2,3,16,64,512]{4,3,2,1,0:T(8,128)(2,1)}) custom-call(bf16[2,3,64,768]{3,2,1,0:T(8,128)(2,1)} %bitcast.113, bf16[2,3,512,768]{3,2,1,0:T(8,128)(2,1)} %all-gather.17.cloned.1.call-done.key_ref, bf16[2,3,512,768]{3,2,1,0:T(8,128)(2,1)} %all-gather.19.cloned.1.call-done.value_ref, ...), custom_call_target="tpu_custom_call" | custom-call | tf_op jit(solution)/shard_map/attend/pallas_call | solution.py:257
  237.2 15.4 %all-gather.21.cloned.1.call-done.zero_ref = bf16[2,384,768]{2,1,0:T(8,128)(2,1)} async-done(((bf16[2,96,768]{2,1,0:T(8,128)(2,1)}), bf16[2,384,768]{2,1,0:T(8,128)(2,1)}) %all-gather.21.cloned.1.call-update) | async-done | bytes 1179664 | tf_op jit(solution)/shard_map/all_gather | solution.py:553
  252.6 29.5 %all-gather.23.cloned.1.call-done.out_w_ref = bf16[768,768]{1,0:T(8,128)(2,1)} async-done(((bf16[192,768]{1,0:T(8,128)(2,1)}), bf16[768,768]{1,0:T(8,128)(2,1)}) %all-gather.23.cloned.1.call-update) | async-done | bytes 1179664 | tf_op jit(solution)/shard_map/all_gather | solution.py:553
  282.0 39.3 %all-gather.27.cloned.1.call-done.tout_ref = bf16[1536,768]{1,0:T(8,128)(2,1)} async-done(((bf16[384,768]{1,0:T(8,128)(2,1)}), bf16[1536,768]{1,0:T(8,128)(2,1)}) %all-gather.27.cloned.1.call-update) | async-done | bytes 2359312 | tf_op jit(solution)/shard_map/all_gather | solution.py:553
  321.4 58.9 %all-gather.25.cloned.1.call-done.tin_ref = bf16[2,768,1536]{2,1,0:T(8,128)(2,1)} async-done(((bf16[2,192,1536]{2,1,0:T(8,128)(2,1)}), bf16[2,768,1536]{2,1,0:T(8,128)(2,1)}) %all-gather.25.cloned.1.call-update) | async-done | bytes 4718608 | tf_op jit(solution)/shard_map/all_gather | solution.py:553
  380.3 21.2 %middle_pass.1 = (bf16[384,768]{1,0:T(8,128)(2,1)}, f32[384,768]{1,0:T(8,128)}, bf16[384,768]{1,0:T(8,128)(2,1)}, bf16[384,768]{1,0:T(8,128)(2,1)}, bf16[384,768...) custom-call(s32[3]{0:T(128)} %pad_add_fusion.meta_ref, ...), custom_call_target="tpu_custom_call" | custom-call | tf_op jit(solution)/shard_map/middle_pass/pallas_call | solution.py:440
  401.5 19.8 %attend_back.1 = (bf16[2,3,64,768]{3,2,1,0:T(8,128)(2,1)}, bf16[2,3,512,768]{3,2,1,0:T(8,128)(2,1)}, bf16[2,3,512,768]{3,2,1,0:T(8,128)(2,1)}, f32[2,16,64,512]{3,2,1,0:T(8,128)}) custom-call(bf16[2,3,16,64,512]{4,3,2,1,0:T(8,128)(2,1)} %get-tuple-element.54.prob_ref, bf16[2,3,64,768]{3,2,1,0:T(8,128)(2,1)} %bitcast.125, bf16[2,3,64,768]{3,2,1,0:T(8,128)(2,1)} %bitcast.114, ...), custom_call_target="tpu_custom_call" | custom-call | tf_op jit(solution)/shard_map/attend_back/pallas_call | solution.py:318
  423.8 2.8 copy.41
  426.7 1.1 copy-done.31
  428.1 1.8 convolution_convert_fusion.3
  430.0 1.2 copy-done.28
  431.2 2.8 convolution_convert_fusion
  434.1 1.2 copy-done.27
  435.4 1.4 fusion
  436.9 1.4 fusion.1
  438.3 2.6 pad_maximum_fusion.1
  440.9 0.9 copy-done.7
  443.0 33.4 %reduce-scatter.8.cloned.1.call-done = bf16[2,3,64,768]{3,2,1,0:T(8,128)(2,1)} async-done(((bf16[2,3,512,768]{3,2,1,0:T(8,128)(2,1)}), bf16[2,3,64,768]{3,2,1,0:T(8,128)(2,1)}) %reduce-scatter.8.cloned.1.call-update) | async-done | bytes 589840 | tf_op jit(solution)/shard_map/reduce_scatter | solution.py:593
  476.4 55.5 %reduce-scatter.10.cloned.1.call-done = bf16[2,3,64,768]{3,2,1,0:T(8,128)(2,1)} async-done(((bf16[2,3,512,768]{3,2,1,0:T(8,128)(2,1)}), bf16[2,3,64,768]{3,2,1,0:T(8,128)(2,1)}) %reduce-scatter.10.cloned.1.call-update) | async-done | bytes 589840 | tf_op jit(solution)/shard_map/reduce_scatter | solution.py:594
  531.9 9.5 %last_pass.1 = (f32[384,768]{1,0:T(8,128)}, bf16[384,768]{1,0:T(8,128)(2,1)}, bf16[384,768]{1,0:T(8,128)(2,1)}, bf16[384,384]{1,0:T(8,128)(2,1)}, f32[8,768]{1,0:T(8,128)}) custom-call(bf16[384,768]{1,0:T(8,128)(2,1)} %bitcast.117, bf16[384,768]{1,0:T(8,128)(2,1)} %bitcast.119, bf16[384,768]{1,0:T(8,128)(2,1)} %bitcast.121, ...), custom_call_target="tpu_custom_call" | custom-call | tf_op jit(solution)/shard_map/last_pass/pallas_call | solution.py:526
  541.4 1.7 fusion.6
  543.6 1.7 pad_maximum_fusion.2
  545.7 0.7 copy-done
  546.6 0.8 fusion.2
  547.7 0.8 fusion.5
  548.7 0.8 fusion.3
  549.8 0.8 fusion.4
  550.6 2.5 pad_maximum_fusion
  553.8 34.6 %all-reduce.8.cloned.1.call-done = bf16[2,384,768]{2,0,1:T(2,128)(2,1)} async-done(((bf16[2,384,768]{2,0,1:T(2,128)(2,1)}), bf16[2,384,768]{2,0,1:T(2,128)(2,1)}) %all-reduce.8.cloned.1.call-update) | async-done | bytes 1179664
  588.4 1.9 constant_dynamic-slice_fusion.1
  590.3 30.3 %reduce-scatter.16.cloned.1.call-done = bf16[192,768]{1,0:T(8,128)(2,1)} async-done(((bf16[768,768]{1,0:T(8,128)(2,1)}), bf16[192,768]{1,0:T(8,128)(2,1)}) %reduce-scatter.16.cloned.1.call-update) | async-done | bytes 294928 | tf_op jit(solution)/shard_map/reduce_scatter | solution.py:608
  620.6 41.3 %reduce-scatter.20.cloned.1.call-done = bf16[384,768]{1,0:T(8,128)(2,1)} async-done(((bf16[1536,768]{1,0:T(8,128)(2,1)}), bf16[384,768]{1,0:T(8,128)(2,1)}) %reduce-scatter.20.cloned.1.call-update) | async-done | bytes 589840 | tf_op jit(solution)/shard_map/reduce_scatter | solution.py:608
  661.9 60.2 %reduce-scatter.18.cloned.1.call-done = bf16[2,192,1536]{2,1,0:T(8,128)(2,1)} async-done(((bf16[2,768,1536]{2,1,0:T(8,128)(2,1)}), bf16[2,192,1536]{2,1,0:T(8,128)(2,1)}) %reduce-scatter.18.cloned.1.call-update) | async-done | bytes 1179664 | tf_op jit(solution)/shard_map/reduce_scatter | solution.py:608
  722.1 41.2 %reduce-scatter.12.cloned.1.call-done = bf16[4,96,768]{2,1,0:T(8,128)(2,1)} async-done(((bf16[4,384,768]{2,1,0:T(8,128)(2,1)}), bf16[4,96,768]{2,1,0:T(8,128)(2,1)}) %reduce-scatter.12.cloned.1.call-update) | async-done | bytes 589840 | tf_op jit(solution)/shard_map/reduce_scatter | solution.py:608
  763.3 60.2 %reduce-scatter.14.cloned.1.call-done = bf16[4,192,768]{2,1,0:T(8,128)(2,1)} async-done(((bf16[4,768,768]{2,1,0:T(8,128)(2,1)}), bf16[4,192,768]{2,1,0:T(8,128)(2,1)}) %reduce-scatter.14.cloned.1.call-update) | async-done | bytes 1179664 | tf_op jit(solution)/shard_map/reduce_scatter | solution.py:608
  823.5 0.7 copy-done.19
  824.3 15.5 %pair_grad.1 = f32[16,128]{1,0:T(8,128)} custom-call(f32[2,16,64,512]{3,2,1,0:T(8,128)} %get-tuple-element.64.dbias_ref, bf16[2,64,512,128]{3,2,1,0:T(8,128)(2,1)} %get-tuple-element.65.low_ref), custom_call_target="tpu_custom_call" | custom-call | tf_op jit(solution)/shard_map/pair_grad/pallas_call | solution.py:150
  839.8 0.7 pad_maximum_fusion.4
  840.5 41.3 %psum.49 = f32[14336]{0:T(1024)S(1)} all-reduce(f32[14336]{0:T(1024)S(1)} %pad_maximum_fusion.4), channel_id=1, replica_groups=mesh['row'=8,'sample'=4] {'row','sample'}, use_global_device_ids=true, to_apply=%region_2.0 | all-reduce | flops 14336 | bytes 114688 | tf_op jit(solution)/shard_map/psum | solution.py:614
  885.1 40.1 %all-reduce.10.cloned.1.call-done = (bf16[2,96,768]{2,0,1:T(2,128)(2,1)}, bf16[4,96,768]{2,1,0:T(8,128)(2,1)}, bf16[4,192,768]{2,1,0:T(8,128)(2,1)}, bf16[192,76...) async-done(((bf16[2,96,768]{2,0,1:T(2,128)(2,1)}, bf16[4,96,768]{2,1,0:T(8,128)(2,1)}, bf16[4,192,768]{2,1,0:T(8,128)(2,1)}, ...) | async-done | bytes 4128784 | tf_op jit(solution)/shard_map/psum | solution.py:609
  925.2 3.0 convert_element_type.86
  928.2 1.7 convert_element_type.91
  929.9 1.1 convert_element_type.76
  931.1 1.1 convert_element_type.93
  932.2 0.9 convert_element_type.88
  933.1 0.9 copy.42
  (136 shorter events, 15.7 us)
Async XLA Ops:
  7.2 1.6 copy-start.22
  7.2 3.5 copy-start.33
  7.2 3.7 copy-start.34
  7.2 15.9 %copy-start.23 = (bf16[2,192]{1,0:T(2,128)(2,1)S(1)}, bf16[2,192]{1,0:T(2,128)(2,1)}, u32[]{:S(2)}) copy-start(bf16[2,192]{1,0:T(2,128)(2,1)} %param.26) | copy-start | bytes 2308
  7.2 23.7 %copy-start.25 = (bf16[2,96]{1,0:T(2,128)(2,1)S(1)}, bf16[2,96]{1,0:T(2,128)(2,1)}, u32[]{:S(2)}) copy-start(bf16[2,96]{1,0:T(2,128)(2,1)} %param.24) | copy-start | bytes 1156
  7.2 42.9 %all-gather.13.cloned.1.call-start = ((), (), s32[]{:S(2)}) async-start(), calls=%async_computation.7 | async-start | bytes 2949120 | tf_op jit(solution)/shard_map/all_gather | solution.py:553
  8.0 101.1 %all-gather.15.cloned.1.call-start = ((), (), s32[]{:S(2)}) async-start(), calls=%async_computation.8 | async-start | bytes 5898240 | tf_op jit(solution)/shard_map/all_gather | solution.py:553
  8.7 163.0 %all-gather.17.cloned.1.call-start = ((), (), s32[]{:S(2)}) async-start(), calls=%async_computation.9 | async-start | bytes 5308416 | tf_op jit(solution)/shard_map/all_gather | solution.py:582
  119.9 104.4 %all-gather.19.cloned.1.call-start = ((), (), s32[]{:S(2)}) async-start(), calls=%async_computation.10 | async-start | bytes 5308416 | tf_op jit(solution)/shard_map/all_gather | solution.py:583
  120.4 2.8 copy-start.21
  120.5 11.6 %copy-start.24 = (bf16[2,192]{1,0:T(2,128)(2,1)S(1)}, bf16[2,192]{1,0:T(2,128)(2,1)}, u32[]{:S(2)}) copy-start(bf16[2,192]{1,0:T(2,128)(2,1)} %param.28) | copy-start | bytes 2308
  120.5 19.5 %copy-start.35 = (s32[2]{0:T(128)S(1)}, s32[2]{0:T(128)}, u32[]{:S(2)}) copy-start(s32[2]{0:T(128)} %param.21) | copy-start | bytes 28
  120.5 132.1 %all-gather.21.cloned.1.call-start = ((), (), s32[]{:S(2)}) async-start(), calls=%async_computation.11 | async-start | bytes 1474560 | tf_op jit(solution)/shard_map/all_gather | solution.py:553
  121.1 161.0 %all-gather.23.cloned.1.call-start = ((), (), s32[]{:S(2)}) async-start(), calls=%async_computation.12 | async-start | bytes 1474560 | tf_op jit(solution)/shard_map/all_gather | solution.py:553
  121.6 199.7 %all-gather.27.cloned.1.call-start = ((), (), s32[]{:S(2)}) async-start(), calls=%async_computation.14 | async-start | bytes 2949120 | tf_op jit(solution)/shard_map/all_gather | solution.py:553
  122.4 257.9 %all-gather.25.cloned.1.call-start = ((), (), s32[]{:S(2)}) async-start(), calls=%async_computation.13 | async-start | bytes 5898240 | tf_op jit(solution)/shard_map/all_gather | solution.py:553
  123.1 353.2 %reduce-scatter.8.cloned.1.call-start = ((), (), s32[]{:S(2)}) async-start(), calls=%async_computation.15 | async-start | bytes 5308416 | tf_op jit(solution)/shard_map/reduce_scatter | solution.py:593
  421.3 110.6 %reduce-scatter.10.cloned.1.call-start = ((), (), s32[]{:S(2)}) async-start(), calls=%async_computation.16 | async-start | bytes 5308416 | tf_op jit(solution)/shard_map/reduce_scatter | solution.py:594
  421.3 1.0 copy-start.1
  421.4 1.1 copy-start.14
  421.9 1.2 copy-start.13
  421.9 166.5 %all-reduce.8.cloned.1.call-start = ((), (), s32[]{:S(2)}) async-start(), calls=%async_computation.22 | async-start | bytes 2359296
  426.7 1.2 copy-start.31
  426.7 1.4 copy-start.32
  426.7 193.9 %reduce-scatter.16.cloned.1.call-start = ((), (), s32[]{:S(2)}) async-start(), calls=%async_computation.19 | async-start | bytes 1474560 | tf_op jit(solution)/shard_map/reduce_scatter | solution.py:608
  428.1 1.9 copy-start.30
  429.9 1.3 copy-start.28
  429.9 232.0 %reduce-scatter.20.cloned.1.call-start = ((), (), s32[]{:S(2)}) async-start(), calls=%async_computation.21 | async-start | bytes 2949120 | tf_op jit(solution)/shard_map/reduce_scatter | solution.py:608
  434.0 1.3 copy-start.27
  434.0 1.4 copy-start.29
  434.0 288.1 %reduce-scatter.18.cloned.1.call-start = ((), (), s32[]{:S(2)}) async-start(), calls=%async_computation.20 | async-start | bytes 5898240 | tf_op jit(solution)/shard_map/reduce_scatter | solution.py:608
  435.4 1.4 copy-start.26
  440.9 1.0 copy-start.7
  440.9 1.2 copy-start.12
  440.9 1.6 copy-start.11
  440.9 322.4 %reduce-scatter.12.cloned.1.call-start = ((), (), s32[]{:S(2)}) async-start(), calls=%async_computation.17 | async-start | bytes 2949120 | tf_op jit(solution)/shard_map/reduce_scatter | solution.py:608
  541.4 1.7 copy-start.8
  541.4 1.8 copy-start.15
  545.3 1.1 copy-start
  545.3 1.3 copy-start.3
  545.3 278.2 %reduce-scatter.14.cloned.1.call-start = ((), (), s32[]{:S(2)}) async-start(), calls=%async_computation.18 | async-start | bytes 5898240 | tf_op jit(solution)/shard_map/reduce_scatter | solution.py:608
  546.6 1.1 copy-start.2
  547.7 1.1 copy-start.4
  548.7 1.1 copy-start.5
  553.1 372.1 %all-reduce.10.cloned.1.call-start = ((), (), s32[]{:S(2)}) async-start(), calls=%async_computation.23 | async-start | bytes 8257536 | tf_op jit(solution)/shard_map/psum | solution.py:609
  823.5 0.7 copy-start.19
  824.3 15.5 %copy-start.20 = (f32[8,768]{1,0:T(8,128)S(1)}, f32[8,768]{1,0:T(8,128)}, u32[]{:S(2)}) copy-start(f32[8,768]{1,0:T(8,128)} %get-tuple-element.63) | copy-start | bytes 73732
  824.3 57.6 %copy-start.18 = (bf16[128,16]{0,1:T(8,128)(2,1)S(1)}, bf16[128,16]{0,1:T(8,128)(2,1)}, u32[]{:S(2)}) copy-start(bf16[128,16]{0,1:T(8,128)(2,1)} %reshape.128) | copy-start | bytes 12292
  925.2 3.0 copy-start.6
  928.2 1.7 copy-start.10
  929.9 1.2 copy-start.9
  931.0 1.2 copy-start.17
  931.1 2.0 copy-start.16
Sparse Core Ops, SparseCore 0:
  9.9 40.1 all-gather.12
  52.0 57.0 all-gather.14
  120.0 51.6 all-gather.16
  173.7 50.5 all-gather.18
  226.0 26.5 all-gather.20
  254.3 27.7 all-gather.22
  283.9 37.4 all-gather.26
  323.2 57.0 all-gather.24
  421.4 54.9 reduce-scatter.7
  478.5 53.3 reduce-scatter.9
  535.6 52.8 all-reduce.7
  592.0 28.5 reduce-scatter.15
  624.5 37.3 reduce-scatter.19
  665.0 57.0 reduce-scatter.17
  725.9 37.3 reduce-scatter.11
  766.4 57.0 reduce-scatter.13
  827.0 98.1 all-reduce.9

commit v2 on v1

--- a/solution.py
+++ b/solution.py
@@ -34,6 +34,618 @@
 
 def params(**extra):
     return pltpu.CompilerParams(vmem_limit_bytes=VMEM_LIMIT, **extra)
+
+
+MESH = pl.DeviceIdType.MESH
+ANY = pl.BlockSpec(memory_space=pl.ANY)
+
+
+class Place:
+    def __init__(self, chips, samples):
+        self.row = lax.axis_index("row")
+        self.chip = self.row // 2
+        self.core = self.row % 2
+        self.sample = lax.axis_index("sample")
+        self.chips, self.samples = chips, samples
+
+    def twin(self):
+        return (self.row + 1 - 2 * self.core, self.sample)
+
+    def peer(self, k):
+        return (self.row, jnp.bitwise_xor(self.sample, k))
+
+    def up(self):
+        return (self.row + 2, self.sample)
+
+    def down(self):
+        return (self.row - 2, self.sample)
+
+    def barrier(self, plane, line):
+        bar = pltpu.get_barrier_semaphore()
+
+        def greet(device):
+            pl.semaphore_signal(bar, inc=1, device_id=device, device_id_type=MESH)
+
+        greet(self.twin())
+        if plane:
+            for k in range(1, self.samples):
+                greet(self.peer(k))
+        if line:
+
+            @pl.when(self.chip > 0)
+            def _():
+                greet(self.down())
+
+            @pl.when(self.chip < self.chips - 1)
+            def _():
+                greet(self.up())
+
+        count = 1 + (self.samples - 1 if plane else 0)
+        if line:
+            count = count + jnp.minimum(self.chip, 1) + jnp.minimum(self.chips - 1 - self.chip, 1)
+        pl.semaphore_wait(bar, count)
+
+
+def send(source, target, send_sem, recv_sem, device):
+    return pltpu.make_async_remote_copy(
+        source, target, send_sem, recv_sem, device_id=device, device_id_type=MESH
+    )
+
+
+def half_of(ref, core):
+    if ref.shape[0] > 1:
+        size = ref.shape[0] // 2
+        return ref.at[pl.ds(core * size, size)]
+    size = ref.shape[1] // 2
+    return ref.at[:, pl.ds(pl.multiple_of(core * size, 16), size)]
+
+
+class PlaneGather:
+    @staticmethod
+    def sems(arrays, samples):
+        dma = pltpu.SemaphoreType.DMA
+        return [dma((arrays, samples))] * 4 + [dma((arrays, 2))] * 2
+
+    def __init__(self, place, shards, fulls, sems):
+        self.place, self.shards, self.fulls = place, shards, fulls
+        self.out, self.come, self.swap_out, self.swap_come, self.hop_out, self.hop_come = sems
+        self.relayed = place.samples == 4
+        self.direct = [1, 2] if self.relayed else list(range(1, place.samples))
+
+    def owner(self, k):
+        return jnp.bitwise_xor(self.place.sample, k)
+
+    def half(self, i, k):
+        return half_of(self.fulls[i].at[self.owner(k)], self.place.core)
+
+    def copy(self, i, k):
+        slot = self.half(i, 0)
+        return send(
+            half_of(self.shards[i], self.place.core), slot, self.out.at[i, k], self.come.at[i, k],
+            self.place.peer(k),
+        )
+
+    def hop(self, i, k):
+        slot = self.half(i, k)
+        size = slot.shape[1] // 2
+        piece = slot.at[:, pl.ds((k - 1) * size, size)]
+        return send(piece, piece, self.hop_out.at[i, k - 1], self.hop_come.at[i, k - 1], self.place.peer(3 - k))
+
+    def swap(self, i, k):
+        slot = self.half(i, k)
+        return send(slot, slot, self.swap_out.at[i, k], self.swap_come.at[i, k], self.place.twin())
+
+    def keep(self, i):
+        return send(
+            self.shards[i], self.fulls[i].at[self.place.sample], self.swap_out.at[i, 0],
+            self.swap_come.at[i, 0], self.place.twin(),
+        )
+
+    def start(self):
+        for i in range(len(self.shards)):
+            for k in self.direct:
+                self.copy(i, k).start()
+            self.keep(i).start()
+
+    def relay(self, i):
+        for k in self.direct:
+            self.copy(i, k).wait_recv()
+            if self.relayed:
+                self.hop(i, k).start()
+            self.swap(i, k).start()
+
+    def settle(self, i):
+        if self.relayed:
+            for k in self.direct:
+                self.hop(i, k).wait_recv()
+            self.swap(i, 3).start()
+
+    def finish(self):
+        for i in range(len(self.shards)):
+            self.keep(i).wait()
+            for k in self.direct:
+                self.copy(i, k).wait_send()
+                if self.relayed:
+                    self.hop(i, k).wait_send()
+            for k in range(1, self.place.samples):
+                self.swap(i, k).wait()
+
+
+class LineSpread:
+    @staticmethod
+    def sems(lines, chips):
+        dma = pltpu.SemaphoreType.DMA
+        return [dma((lines, chips))] * 6
+
+    def __init__(self, place, line, slot, sems):
+        self.place, self.line, self.slot = place, line, slot
+        self.up_out, self.up_come, self.down_out, self.down_come, self.swap_out, self.swap_come = sems
+
+    def step(self, upward, t):
+        place, last = self.place, self.place.chips - 1
+        z = place.chip
+        if upward:
+            out_chip, has_out = z - t + 1, (z >= t - 1) & (z < last)
+            in_chip, has_in = z - t, z >= t
+            sems, device = (self.up_out, self.up_come), place.up()
+        else:
+            out_chip, has_out = z + t - 1, (z + t - 1 <= last) & (z > 0)
+            in_chip, has_in = z + t, z + t <= last
+            sems, device = (self.down_out, self.down_come), place.down()
+        make = lambda chip: send(
+            self.slot(chip), self.slot(chip),
+            sems[0].at[self.line, t], sems[1].at[self.line, t], device,
+        )
+        return (has_out, lambda: make(out_chip)), (has_in, in_chip, lambda: make(in_chip))
+
+    def hand_over(self, chip):
+        slot = self.slot(chip)
+        return send(
+            slot, slot, self.swap_out.at[self.line, chip], self.swap_come.at[self.line, chip],
+            self.place.twin(),
+        )
+
+    def depart(self, t):
+        for upward in (True, False):
+            (has_out, copy), _ = self.step(upward, t)
+
+            @pl.when(has_out)
+            def _():
+                copy().start()
+
+    def advance(self, t):
+        for upward in (True, False):
+            _, (has_in, chip, copy) = self.step(upward, t)
+
+            @pl.when(has_in)
+            def _():
+                copy().wait_recv()
+
+        if t + 1 < self.place.chips:
+            self.depart(t + 1)
+        for upward in (True, False):
+            _, (has_in, chip, copy) = self.step(upward, t)
+
+            @pl.when(has_in)
+            def _():
+                self.hand_over(chip).start()
+
+    def finish(self):
+        for t in range(1, self.place.chips):
+            for upward in (True, False):
+                (has_out, copy), (has_in, chip, _) = self.step(upward, t)
+
+                @pl.when(has_out)
+                def _():
+                    copy().wait_send()
+
+                @pl.when(has_in)
+                def _():
+                    self.hand_over(chip).wait()
+
+
+class LineReduce:
+    @staticmethod
+    def sems(lines, chips):
+        dma = pltpu.SemaphoreType.DMA
+        return [dma((lines, chips))] * 4
+
+    def __init__(self, place, line, slot, up_buf, down_buf, sems):
+        self.place, self.line, self.slot = place, line, slot
+        self.bufs = (up_buf, down_buf)
+        self.up_out, self.up_come, self.down_out, self.down_come = sems
+
+    def step(self, upward, t):
+        place, last = self.place, self.place.chips - 1
+        z, distance = place.chip, place.chips - t
+        buf = self.bufs[0 if upward else 1]
+        if upward:
+            block, has_out, has_before = z + distance, z + distance <= last, z > 0
+            has_in = (z > 0) & (z - 1 + distance <= last)
+            sems, device = (self.up_out, self.up_come), place.up()
+        else:
+            block, has_out, has_before = z - distance, z - distance >= 0, z < last
+            has_in = (z < last) & (z + 1 - distance >= 0)
+            sems, device = (self.down_out, self.down_come), place.down()
+        copy = lambda chip: send(
+            self.slot(chip), buf.at[self.line, t],
+            sems[0].at[self.line, t], sems[1].at[self.line, t], device,
+        )
+        return block, has_out, has_before, has_in, copy, buf
+
+    def advance(self, t):
+        for upward in (True, False):
+            block, has_out, has_before, _, copy, buf = self.step(upward, t)
+            before = self.step(upward, t - 1)[4] if t > 1 else None
+
+            @pl.when(has_out)
+            def _():
+                if t > 1:
+
+                    @pl.when(has_before)
+                    def _():
+                        before(block).wait_recv()
+                        slot = self.slot(block)
+                        slot[...] = (
+                            slot[...].astype(F32) + buf[self.line, t - 1].astype(F32)
+                        ).astype(slot.dtype)
+
+                copy(block).start()
+
+    def finish(self):
+        last_step = self.place.chips - 1
+        slot = self.slot(self.place.chip)
+        for upward in (True, False):
+            _, _, _, has_in, copy, buf = self.step(upward, last_step)
+
+            @pl.when(has_in)
+            def _():
+                copy(self.place.chip).wait_recv()
+                slot[...] = (
+                    slot[...].astype(F32) + buf[self.line, last_step].astype(F32)
+                ).astype(slot.dtype)
+
+        for t in range(1, self.place.chips):
+            for upward in (True, False):
+                block, has_out, _, _, copy, _ = self.step(upward, t)
+
+                @pl.when(has_out)
+                def _():
+                    copy(block).wait_send()
+
+
+class RowGather:
+    @staticmethod
+    def sems(lines, chips):
+        dma = pltpu.SemaphoreType.DMA
+        return [dma((lines, 2))] * 3 + LineSpread.sems(lines, chips)
+
+    def __init__(self, place, part, full, line, sems):
+        self.place, self.part, self.full, self.index = place, part, full, line
+        self.spot = (line // part.shape[2], line % part.shape[2])
+        self.local, self.swap_out, self.swap_come = sems[:3]
+        self.rows = part.shape[3]
+        self.line = LineSpread(place, line, self.chip_slot, sems[3:])
+
+    def chip_slot(self, chip):
+        size = 2 * self.rows
+        rows = pl.ds(pl.multiple_of(chip * size, size), size)
+        return self.full.at[(self.place.core,) + self.spot + (rows,)]
+
+    def own_slot(self, role):
+        rows = pl.ds(pl.multiple_of(self.place.row * self.rows, self.rows), self.rows)
+        return self.full.at[(role,) + self.spot + (rows,)]
+
+    def keep(self, role):
+        return pltpu.make_async_copy(
+            self.part.at[(role,) + self.spot], self.own_slot(role), self.local.at[self.index, role]
+        )
+
+    def first_swap(self, role):
+        return send(
+            self.part.at[(role,) + self.spot], self.own_slot(role),
+            self.swap_out.at[self.index, role], self.swap_come.at[self.index, role], self.place.twin(),
+        )
+
+    def start(self):
+        for role in range(2):
+            self.keep(role).start()
+            self.first_swap(role).start()
+
+    def begin(self):
+        for role in range(2):
+            self.keep(role).wait()
+            self.first_swap(role).wait()
+        self.line.depart(1)
+
+
+def gather_kernel(arrays, chips, samples, *refs):
+    shards, fulls = refs[:arrays], refs[arrays : 2 * arrays]
+    place = Place(chips, samples)
+    move = PlaneGather(place, shards, fulls, refs[2 * arrays :])
+    place.barrier(True, False)
+    move.start()
+    for i in range(arrays):
+        move.relay(i)
+        if i:
+            move.settle(i - 1)
+    move.settle(arrays - 1)
+    move.finish()
+
+
+def gather_weights(shards, collective_id):
+    samples, chips = lax.axis_size("sample"), lax.axis_size("row") // 2
+    count = len(shards)
+    return pl.pallas_call(
+        functools.partial(gather_kernel, count, chips, samples),
+        in_specs=[ANY] * count,
+        out_specs=[ANY] * count,
+        out_shape=[jax.ShapeDtypeStruct((samples,) + s.shape, s.dtype) for s in shards],
+        scratch_shapes=PlaneGather.sems(count, samples),
+        compiler_params=pltpu.CompilerParams(collective_id=collective_id, has_side_effects=True),
+        name="gather_weights",
+    )(*shards)
+
+
+def gather_rows_kernel(chips, samples, part_ref, full_ref, *sems):
+    place = Place(chips, samples)
+    lines = part_ref.shape[1] * part_ref.shape[2]
+    moves = [RowGather(place, part_ref, full_ref, line, sems) for line in range(lines)]
+    place.barrier(False, True)
+    for move in moves:
+        move.start()
+    for move in moves:
+        move.begin()
+    for t in range(1, chips):
+        for move in moves:
+            move.line.advance(t)
+    for move in moves:
+        move.line.finish()
+
+
+def gather_rows(part, collective_id):
+    samples, chips = lax.axis_size("sample"), lax.axis_size("row") // 2
+    two, complexes, own, rows, width = part.shape
+    full = (two, complexes, own, rows * 2 * chips, width)
+    return pl.pallas_call(
+        functools.partial(gather_rows_kernel, chips, samples),
+        in_specs=[pl.BlockSpec(memory_space=pltpu.VMEM)],
+        out_specs=ANY,
+        out_shape=jax.ShapeDtypeStruct(full, part.dtype),
+        scratch_shapes=RowGather.sems(complexes * own, chips),
+        compiler_params=params(collective_id=collective_id, has_side_effects=True),
+        name="gather_rows",
+    )(part)
+
+
+class RowReduce:
+    @staticmethod
+    def scratch(complexes, samples_own, length, rows, width, chips):
+        dma = pltpu.SemaphoreType.DMA
+        hop = pltpu.VMEM((complexes, chips, samples_own, 2 * rows, width), BF16)
+        return [
+            pltpu.VMEM((complexes, samples_own, length, width), BF16), hop, hop,
+        ] + [dma((complexes,))] * 5 + LineReduce.sems(complexes, chips)
+
+    def __init__(self, place, part, own, which, scratch):
+        self.place, self.part, self.own, self.which = place, part, own, which
+        self.sums, up_buf, down_buf = scratch[:3]
+        self.swap_out, self.swap_come, self.last_out, self.last_come, self.keep_sem = scratch[3:8]
+        self.rows = own.shape[3]
+        self.line = LineReduce(place, which, self.chip_slot, up_buf, down_buf, scratch[8:])
+
+    def chip_slot(self, chip):
+        size = 2 * self.rows
+        return self.sums.at[self.which, :, pl.ds(pl.multiple_of(chip * size, size), size)]
+
+    def first_swap(self):
+        return send(
+            self.part.at[1 - self.place.core, self.which], self.sums.at[self.which],
+            self.swap_out.at[self.which], self.swap_come.at[self.which], self.place.twin(),
+        )
+
+    def begin(self):
+        self.first_swap().wait_recv()
+        for sample in range(self.part.shape[2]):
+            mine = self.part[self.place.core, self.which, sample].astype(F32)
+            self.sums[self.which, sample] = (
+                mine + self.sums[self.which, sample].astype(F32)
+            ).astype(BF16)
+
+    def result(self, core):
+        spot = self.place.row - self.place.core + core
+        spot = pl.ds(pl.multiple_of(spot * self.rows, self.rows), self.rows)
+        return self.sums.at[self.which, :, spot]
+
+    def last_copies(self):
+        target = self.own.at[self.place.core, self.which]
+        return (
+            send(
+                self.result(1 - self.place.core), target,
+                self.last_out.at[self.which], self.last_come.at[self.which], self.place.twin(),
+            ),
+            pltpu.make_async_copy(self.result(self.place.core), target, self.keep_sem.at[self.which]),
+        )
+
+    def finish(self):
+        self.line.finish()
+        for copy in self.last_copies():
+            copy.start()
+
+    def drain(self):
+        self.first_swap().wait_send()
+        for copy in self.last_copies():
+            copy.wait()
+
+
+def reduce_rows_kernel(chips, samples, part_ref, own_ref, *scratch):
+    place = Place(chips, samples)
+    moves = [
+        RowReduce(place, part_ref, own_ref, which, scratch) for which in range(part_ref.shape[1])
+    ]
+    place.barrier(False, True)
+    for move in moves:
+        move.first_swap().start()
+    for move in moves:
+        move.begin()
+        move.line.advance(1)
+    for t in range(2, chips):
+        for move in moves:
+            move.line.advance(t)
+    for move in moves:
+        move.finish()
+    for move in moves:
+        move.drain()
+
+
+def reduce_rows(part, collective_id):
+    samples, chips = lax.axis_size("sample"), lax.axis_size("row") // 2
+    two, complexes, own, length, width = part.shape
+    rows = length // (2 * chips)
+    return pl.pallas_call(
+        functools.partial(reduce_rows_kernel, chips, samples),
+        in_specs=[pl.BlockSpec(memory_space=pltpu.VMEM)],
+        out_specs=ANY,
+        out_shape=jax.ShapeDtypeStruct((two, complexes, own, rows, width), part.dtype),
+        scratch_shapes=RowReduce.scratch(complexes, own, length, rows, width, chips),
+        compiler_params=params(collective_id=collective_id, has_side_effects=True),
+        name="reduce_rows",
+    )(part)
+
+
+class PlaneReduce:
+    @staticmethod
+    def scratch(samples, rows, width):
+        dma = pltpu.SemaphoreType.DMA
+        half = rows // 2
+        return [
+            pltpu.VMEM((samples, half, width), BF16), pltpu.VMEM((samples, half, width), BF16),
+        ] + [dma((samples,))] * 4
+
+    def __init__(self, place, grads, plane, scratch):
+        self.place, self.grads, self.plane = place, grads, plane
+        self.sums, self.come_buf, self.swap_out, self.swap_come, self.out, self.come = scratch
+        self.half = grads.shape[1] // 2
+
+    def shard(self, k):
+        return jnp.bitwise_xor(self.place.sample, k)
+
+    def half_rows(self, core):
+        return pl.ds(pl.multiple_of(core * self.half, 16), self.half)
+
+    def swap(self, k):
+        return send(
+            self.grads.at[self.shard(k), self.half_rows(1 - self.place.core)],
+            self.sums.at[self.shard(k)],
+            self.swap_out.at[k], self.swap_come.at[k], self.place.twin(),
+        )
+
+    def copy(self, k):
+        return send(
+            self.sums.at[self.shard(k)], self.come_buf.at[k], self.out.at[k], self.come.at[k],
+            self.place.peer(k),
+        )
+
+    def order(self):
+        return list(range(1, self.place.samples)) + [0]
+
+    def start(self):
+        for k in self.order():
+            self.swap(k).start()
+
+    def depart(self, k):
+        self.swap(k).wait_recv()
+        mine = self.grads[self.shard(k), self.half_rows(self.place.core)].astype(F32)
+        slot = self.sums.at[self.shard(k)]
+        slot[...] = (mine + slot[...].astype(F32)).astype(BF16)
+        if k:
+            self.copy(k).start()
+
+    def finish(self):
+        value = self.sums[self.place.sample].astype(F32)
+        for k in range(1, self.place.samples):
+            self.copy(k).wait_recv()
+            value = value + self.come_buf[k].astype(F32)
+        self.plane[...] = value.astype(BF16)
+
+    def drain(self):
+        for k in self.order():
+            self.swap(k).wait_send()
+            if k:
+                self.copy(k).wait_send()
+
+
+class LineTotal:
+    @staticmethod
+    def scratch(rows, width, chips):
+        hop = pltpu.VMEM((1, chips, rows // 2 // chips, width), BF16)
+        return [hop, hop] + LineReduce.sems(1, chips) + LineSpread.sems(1, chips)
+
+    def __init__(self, place, plane, total, scratch):
+        self.place, self.plane, self.total = place, plane, total
+        self.half = total.shape[0] // 2
+        self.size = self.half // place.chips
+        self.reduce = LineReduce(place, 0, self.block, scratch[0], scratch[1], scratch[2:6])
+        self.spread = LineSpread(place, 0, self.slot, scratch[6:])
+
+    def block(self, chip):
+        return self.plane.at[pl.ds(pl.multiple_of(chip * self.size, 16), self.size)]
+
+    def slot(self, chip):
+        start = self.place.core * self.half + chip * self.size
+        return self.total.at[pl.ds(pl.multiple_of(start, 16), self.size)]
+
+    def turn(self):
+        self.reduce.finish()
+        own = self.slot(self.place.chip)
+        own[...] = self.block(self.place.chip)[...]
+        self.spread.depart(1)
+        self.spread.hand_over(self.place.chip).start()
+
+    def finish(self):
+        self.spread.finish()
+        self.spread.hand_over(self.place.chip).wait()
+
+
+def reduce_grads_kernel(chips, samples, grads_ref, total_ref, *scratch):
+    place = Place(chips, samples)
+    count = len(PlaneReduce.scratch(samples, 32, 128))
+    plane_buf = scratch[0]
+    plane = PlaneReduce(place, grads_ref, plane_buf, scratch[1 : 1 + count])
+    line = LineTotal(place, plane_buf, total_ref, scratch[1 + count :])
+    place.barrier(True, True)
+    plane.start()
+    for k in plane.order():
+        plane.depart(k)
+    plane.finish()
+    for t in range(1, chips):
+        line.reduce.advance(t)
+    line.turn()
+    for t in range(1, chips):
+        line.spread.advance(t)
+    line.finish()
+    plane.drain()
+
+
+def reduce_grads(grads, collective_id):
+    chips = lax.axis_size("row") // 2
+    samples, rows, width = grads.shape
+    return pl.pallas_call(
+        functools.partial(reduce_grads_kernel, chips, samples),
+        in_specs=[pl.BlockSpec(memory_space=pltpu.VMEM)],
+        out_specs=pl.BlockSpec(memory_space=pltpu.VMEM),
+        out_shape=jax.ShapeDtypeStruct((rows, width), BF16),
+        scratch_shapes=[pltpu.VMEM((rows // 2, width), BF16)]
+        + PlaneReduce.scratch(samples, rows, width)
+        + LineTotal.scratch(rows, width, chips),
+        compiler_params=params(collective_id=collective_id, has_side_effects=True),
+        name="reduce_grads",
+    )(grads)
+
+
+def joined(ref, which=0):
+    samples, _, rows, cols = ref.shape
+    return ref[:, which].reshape(samples * rows, cols)
 
 
 def head_windows(heads, head_dim):
@@ -171,14 +783,14 @@
     def _():
         cond, _ = center_rows(single_ref[...].astype(F32))
         cond = (cond * gain_ref[0:1].astype(F32)).astype(BF16)
-        pre = dot(cond, ada_ref[0]) + bias_ref[0:1].astype(F32)
-        shift = dot(cond, ada_ref[1])
+        pre = dot(cond, joined(ada_ref, 0)) + bias_ref[0:1].astype(F32)
+        shift = dot(cond, joined(ada_ref, 1))
         normed, _ = center_rows(tok_ref[...].astype(F32))
         normed_in = (jax.nn.sigmoid(pre) * normed + shift).astype(BF16)
         normed_ref[...] = normed_in
         hold_ref[...] = normed_in
 
-    result = dot(hold_ref[...], attn_ref[0])
+    result = dot(hold_ref[...], joined(attn_ref))
 
     @pl.when(which == 0)
     def _():
@@ -204,9 +816,9 @@
             whole((rows, width)),
             whole((rows, cond)),
             whole((2, cond)),
-            pl.BlockSpec((2, cond, width), lambda w: (0, 0, 0)),
+            pl.BlockSpec((ada.shape[0], 2) + ada.shape[2:], lambda w: (0, 0, 0, 0)),
             whole((2, width)),
-            pl.BlockSpec((1, width, width), lambda w: (w, 0, 0)),
+            pl.BlockSpec((attn.shape[0], 1) + attn.shape[2:], lambda w: (0, w, 0, 0)),
             whole((1, width)),
         ],
         out_specs=[
@@ -227,9 +839,9 @@
     )(tok, single, gain, ada, ada_bias, attn, query_bias.reshape(1, width))
 
 
-def attend_kernel(heads, query_ref, key_ref, value_ref, bias_ref, out_ref, prob_ref):
+def attend_kernel(heads, query_ref, keyval_ref, bias_ref, out_ref, prob_ref):
     rows, width = query_ref.shape[2], query_ref.shape[3]
-    length = key_ref.shape[2]
+    length = keyval_ref.shape[3]
     head_dim = width // heads
     scale = head_dim ** (-0.5)
     parts = []
@@ -237,29 +849,28 @@
         count = len(inside)
         lanes = slice(start, start + 256)
         stacked = stack_heads(query_ref[0, 0, :, lanes], start, inside, head_dim)
-        scores = dot_nt(stacked, key_ref[0, 0, :, lanes]) * scale
+        scores = dot_nt(stacked, keyval_ref[0, 0, 0, :, lanes]) * scale
         bias = bias_ref[0, inside[0] : inside[-1] + 1].reshape(count * rows, length)
         scores = scores + bias
         weight = jnp.exp(scores - jnp.max(scores, axis=-1, keepdims=True))
         prob = weight * (1.0 / jnp.sum(weight, axis=-1, keepdims=True))
         low = prob.astype(BF16)
         prob_ref[0, 0, inside[0] : inside[-1] + 1] = low.reshape(count, rows, length)
-        mixed = dot(low, value_ref[0, 0, :, lanes])
+        mixed = dot(low, keyval_ref[1, 0, 0, :, lanes])
         parts.append((start, unstack_heads(mixed, start, inside, head_dim)))
     out_ref[0, 0] = join_windows(parts, width)
 
 
-def attend(query, key, value, bias):
+def attend(query, keyval, bias):
     complexes, samples, rows, width = query.shape
     heads, length = bias.shape[1], bias.shape[3]
     own = pl.BlockSpec((1, 1, rows, width), lambda c, s: (c, s, 0, 0))
-    full = pl.BlockSpec((1, 1, length, width), lambda c, s: (c, s, 0, 0))
+    full = pl.BlockSpec((2, 1, 1, length, width), lambda c, s: (0, c, s, 0, 0))
     return pl.pallas_call(
         functools.partial(attend_kernel, heads),
         grid=(complexes, samples),
         in_specs=[
             own,
-            full,
             full,
             pl.BlockSpec((1, heads, rows, length), lambda c, s: (c, 0, 0, 0)),
         ],
@@ -273,14 +884,14 @@
         ],
         compiler_params=params(),
         name="attend",
-    )(query, key, value, bias)
+    )(query, keyval, bias)
 
 
 def attend_back_kernel(
-    heads, prob_ref, grad_ref, query_ref, key_ref, value_ref, dq_ref, dk_ref, dv_ref, dbias_ref
+    heads, prob_ref, grad_ref, query_ref, keyval_ref, dq_ref, dkeyval_ref, dbias_ref
 ):
     rows, width = query_ref.shape[2], query_ref.shape[3]
-    length = key_ref.shape[2]
+    length = keyval_ref.shape[3]
     head_dim = width // heads
     scale = head_dim ** (-0.5)
 
@@ -297,24 +908,24 @@
         span = slice(inside[0], inside[-1] + 1)
         low = prob_ref[0, 0, span].reshape(count * rows, length)
         prob = low.astype(F32)
-        dprob = dot_nt(grads, value_ref[0, 0, :, lanes])
+        dprob = dot_nt(grads, keyval_ref[1, 0, 0, :, lanes])
         inner = jnp.sum(prob * dprob, axis=-1, keepdims=True)
         dscore = (prob * (dprob - inner)).astype(BF16)
         dbias_ref[0, span] += dscore.astype(F32).reshape(count, rows, length)
-        mixed = dot(dscore, key_ref[0, 0, :, lanes])
+        mixed = dot(dscore, keyval_ref[0, 0, 0, :, lanes])
         dq_parts.append((start, unstack_heads(mixed, start, inside, head_dim)))
         dk_parts.append((start, dot_tn(dscore, queries)))
         dv_parts.append((start, dot_tn(low, grads)))
     dq_ref[0, 0] = (join_windows(dq_parts, width) * scale).astype(BF16)
-    dk_ref[0, 0] = (join_windows(dk_parts, width) * scale).astype(BF16)
-    dv_ref[0, 0] = join_windows(dv_parts, width).astype(BF16)
-
-
-def attend_back(prob, grad, query, key, value):
+    dkeyval_ref[0, 0, 0] = (join_windows(dk_parts, width) * scale).astype(BF16)
+    dkeyval_ref[1, 0, 0] = join_windows(dv_parts, width).astype(BF16)
+
+
+def attend_back(prob, grad, query, keyval):
     complexes, samples, rows, width = query.shape
     heads, length = prob.shape[2], prob.shape[4]
     own = pl.BlockSpec((1, 1, rows, width), lambda c, s: (c, s, 0, 0))
-    full = pl.BlockSpec((1, 1, length, width), lambda c, s: (c, s, 0, 0))
+    full = pl.BlockSpec((2, 1, 1, length, width), lambda c, s: (0, c, s, 0, 0))
     return pl.pallas_call(
         functools.partial(attend_back_kernel, heads),
         grid=(complexes, samples),
@@ -323,23 +934,20 @@
             own,
             own,
             full,
-            full,
         ],
         out_specs=[
             own,
-            full,
             full,
             pl.BlockSpec((1, heads, rows, length), lambda c, s: (c, 0, 0, 0)),
         ],
         out_shape=[
             jax.ShapeDtypeStruct((complexes, samples, rows, width), BF16),
-            jax.ShapeDtypeStruct((complexes, samples, length, width), BF16),
-            jax.ShapeDtypeStruct((complexes, samples, length, width), BF16),
+            jax.ShapeDtypeStruct((2, complexes, samples, length, width), BF16),
             jax.ShapeDtypeStruct((complexes, heads, rows, length), F32),
         ],
         compiler_params=params(),
         name="attend_back",
-    )(prob, grad, query, key, value)
+    )(prob, grad, query, keyval)
 
 
 def middle_kernel(
@@ -360,24 +968,24 @@
     single = single_ref[...]
     gated = (att * gate).astype(BF16)
     gated_ref[...] = gated
-    branch = dot(gated, out_w_ref[...])
-    attn_zero = jax.nn.sigmoid(dot(single, zero_ref[0]) + zero_bias_ref[0:1].astype(F32))
+    branch = dot(gated, joined(out_w_ref))
+    attn_zero = jax.nn.sigmoid(dot(single, joined(zero_ref, 0)) + zero_bias_ref[0:1].astype(F32))
     middle = tok_ref[...].astype(F32) + valid * attn_zero * branch
     cond, _ = center_rows(single.astype(F32))
     tcond = (cond * gain_ref[1:2].astype(F32)).astype(BF16)
     tcond_ref[...] = tcond
-    scale = jax.nn.sigmoid(dot(tcond, ada_ref[0]) + ada_bias_ref[1:2].astype(F32))
-    shift = dot(tcond, ada_ref[1])
+    scale = jax.nn.sigmoid(dot(tcond, joined(ada_ref, 0)) + ada_bias_ref[1:2].astype(F32))
+    shift = dot(tcond, joined(ada_ref, 1))
     normed, rstd = center_rows(middle)
     tinput = (scale * normed + shift).astype(BF16)
     tinput_ref[...] = tinput
-    first = dot(tinput, tin_ref[0])
-    second = dot(tinput, tin_ref[1])
+    first = dot(tinput, joined(tin_ref, 0))
+    second = dot(tinput, joined(tin_ref, 1))
     sig = jax.nn.sigmoid(first)
     hidden = (first * sig * second).astype(BF16)
     hidden_ref[...] = hidden
-    tbranch = dot(hidden, tout_ref[...])
-    trans_zero = jax.nn.sigmoid(dot(single, zero_ref[1]) + zero_bias_ref[1:2].astype(F32))
+    tbranch = dot(hidden, joined(tout_ref))
+    trans_zero = jax.nn.sigmoid(dot(single, joined(zero_ref, 1)) + zero_bias_ref[1:2].astype(F32))
     out_ref[...] = (middle + valid * trans_zero * tbranch).astype(BF16)
     grad_out = cot_ref[...].astype(F32)
     gated_out = grad_out * valid
@@ -385,12 +993,12 @@
     dtbranch_ref[...] = dtbranch
     dzb = (gated_out * tbranch * trans_zero * (1.0 - trans_zero)).astype(BF16)
     dzb_ref[...] = dzb
-    dhidden = dot_nt(dtbranch, tout_ref[...])
+    dhidden = dot_nt(dtbranch, joined(tout_ref))
     dfirst = (dhidden * second * sig * (1.0 + first * (1.0 - sig))).astype(BF16)
     dsecond = (dhidden * first * sig).astype(BF16)
     dfirst_ref[...] = dfirst
     dsecond_ref[...] = dsecond
-    dtin = (dot_nt(dfirst, tin_ref[0]) + dot_nt(dsecond, tin_ref[1])).astype(BF16)
+    dtin = (dot_nt(dfirst, joined(tin_ref, 0)) + dot_nt(dsecond, joined(tin_ref, 1))).astype(BF16)
     dtin_ref[...] = dtin
     dtin_full = dtin.astype(F32)
     dtpre = (dtin_full * normed * scale * (1.0 - scale)).astype(BF16)
@@ -400,13 +1008,13 @@
     tail = tail - normed * jnp.mean(grad_norm * normed, axis=-1, keepdims=True)
     dmid = grad_out + tail * rstd
     dmid_ref[...] = dmid
-    dtcond = dot_nt(dtpre, ada_ref[0]) + dot_nt(dtin, ada_ref[1])
+    dtcond = dot_nt(dtpre, joined(ada_ref, 0)) + dot_nt(dtin, joined(ada_ref, 1))
     gated_mid = dmid * valid
     dabranch = (gated_mid * attn_zero).astype(BF16)
     dabranch_ref[...] = dabranch
     dza = (gated_mid * branch * attn_zero * (1.0 - attn_zero)).astype(BF16)
     dza_ref[...] = dza
-    dgated = dot_nt(dabranch, out_w_ref[...])
+    dgated = dot_nt(dabranch, joined(out_w_ref))
     datt_ref[...] = (dgated * gate).astype(BF16)
     dglogit_ref[...] = (dgated * att * gate * (1.0 - gate)).astype(BF16)
 
@@ -428,7 +1036,7 @@
 ):
     rows, width = tok.shape
     narrow = single.shape[1]
-    hidden = trans_out.shape[0]
+    hidden = trans_out.shape[0] * trans_out.shape[2]
     part = rows // complexes
     wide = pl.BlockSpec((part, width), lambda c, m: (c, 0))
     slim = pl.BlockSpec((part, narrow), lambda c, m: (c, 0))
@@ -445,7 +1053,10 @@
             in_specs=[
                 wide, wide, wide, slim, wide,
                 once(gain.shape),
-                pl.BlockSpec((2, narrow, width), lambda c, m: (1, 0, 0), pipeline_mode=pl.Buffered(1)),
+                pl.BlockSpec(
+                    (ada.shape[0], 2) + ada.shape[2:], lambda c, m: (0, 1, 0, 0),
+                    pipeline_mode=pl.Buffered(1),
+                ),
                 once(ada_bias.shape),
                 once(zero.shape),
                 once(zero_bias.shape),
@@ -474,7 +1085,7 @@
 
 
 def last_kernel(
-    dquery_ref, dkey_ref, dvalue_ref, dglogit_ref, tok_ref, single_ref, dmid_ref,
+    dquery_ref, dkeyval_ref, dglogit_ref, tok_ref, single_ref, dmid_ref,
     gain_ref, ada_ref, ada_bias_ref, attn_ref,
     tgrad_ref, dnormed_ref, dapre_ref, cond_ref, small_ref, acc_ref,
 ):
@@ -482,24 +1093,24 @@
 
     @pl.when(which == 0)
     def _():
-        acc_ref[...] = dot_nt(dquery_ref[...], attn_ref[0])
+        acc_ref[...] = dot_nt(dquery_ref[...], joined(attn_ref))
 
     @pl.when(which == 1)
     def _():
-        acc_ref[...] += dot_nt(dkey_ref[...], attn_ref[0])
+        acc_ref[...] += dot_nt(dkeyval_ref[0], joined(attn_ref))
 
     @pl.when(which == 2)
     def _():
-        acc_ref[...] += dot_nt(dvalue_ref[...], attn_ref[0])
+        acc_ref[...] += dot_nt(dkeyval_ref[1], joined(attn_ref))
 
     @pl.when(which == 3)
     def _():
-        dnormed = (acc_ref[...] + dot_nt(dglogit_ref[...], attn_ref[0])).astype(BF16)
+        dnormed = (acc_ref[...] + dot_nt(dglogit_ref[...], joined(attn_ref))).astype(BF16)
         dnormed_ref[...] = dnormed
         cond, _ = center_rows(single_ref[...].astype(F32))
         cond_low = (cond * gain_ref[0:1].astype(F32)).astype(BF16)
         cond_ref[...] = cond_low
-        scale = jax.nn.sigmoid(dot(cond_low, ada_ref[0]) + ada_bias_ref[0:1].astype(F32))
+        scale = jax.nn.sigmoid(dot(cond_low, joined(ada_ref, 0)) + ada_bias_ref[0:1].astype(F32))
         normed, rstd = center_rows(tok_ref[...].astype(F32))
         full = dnormed.astype(F32)
         dapre = (full * normed * scale * (1.0 - scale)).astype(BF16)
@@ -508,7 +1119,7 @@
         tail = grad_norm - jnp.mean(grad_norm, axis=-1, keepdims=True)
         tail = tail - normed * jnp.mean(grad_norm * normed, axis=-1, keepdims=True)
         tgrad_ref[...] = dmid_ref[...] + tail * rstd
-        dcond = dot_nt(dapre, ada_ref[0]) + dot_nt(dnormed, ada_ref[1])
+        dcond = dot_nt(dapre, joined(ada_ref, 0)) + dot_nt(dnormed, joined(ada_ref, 1))
         narrow = cond.shape[1]
         total = lambda value: jnp.sum(value.astype(F32), axis=0, keepdims=True)
         small_ref[...] = jnp.zeros_like(small_ref)
@@ -517,7 +1128,7 @@
         small_ref[2:3, 0:narrow] = total(dcond * cond)
 
 
-def last_pass(dquery, dkey, dvalue, dglogit, tok, single, dmid, gain, ada, ada_bias, attn):
+def last_pass(dquery, dkeyval, dglogit, tok, single, dmid, gain, ada, ada_bias, attn):
     rows, width = tok.shape
     narrow = single.shape[1]
     whole = lambda shape: pl.BlockSpec(shape, lambda w: (0,) * len(shape))
@@ -527,11 +1138,11 @@
         last_kernel,
         grid=(4,),
         in_specs=[
-            wide, wide, wide, wide, wide, whole((rows, narrow)), wide,
+            wide, whole(dkeyval.shape), wide, wide, whole((rows, narrow)), wide,
             whole(gain.shape),
-            pl.BlockSpec((2, narrow, width), lambda w: (0, 0, 0)),
+            pl.BlockSpec((ada.shape[0], 2) + ada.shape[2:], lambda w: (0, 0, 0, 0)),
             whole(ada_bias.shape),
-            pl.BlockSpec((1, width, width), lambda w: (w, 0, 0)),
+            pl.BlockSpec((attn.shape[0], 1) + attn.shape[2:], lambda w: (0, w, 0, 0)),
         ],
         out_specs=[wide, wide, wide, whole((rows, narrow)), whole((8, width))],
         out_shape=[
@@ -541,17 +1152,92 @@
         scratch_shapes=[pltpu.VMEM((rows, width), F32)],
         compiler_params=params(),
         name="last_pass",
-    )(dquery, dkey, dvalue, dglogit, tok, single, dmid, gain, ada, ada_bias, attn)
-
-
-def weight_grad(left, grads):
-    return [dot_tn(left, grad).astype(BF16) for grad in grads]
-
-
-def gather_weights(shards, axes):
-    return [
-        lax.all_gather(shard, "sample", axis=axis, tiled=True) for shard, axis in zip(shards, axes)
+    )(dquery, dkeyval, dglogit, tok, single, dmid, gain, ada, ada_bias, attn)
+
+
+def grad_rows(samples, chips, parts):
+    unit = 32 * chips
+    return -(-sum(parts) // unit) * unit
+
+
+def store_grads(out_ref, start, left, grads):
+    samples, _, width = out_ref.shape
+    turned = left.T
+    rows = turned.shape[0] // samples
+    for grad in grads:
+        value = dot(turned, grad).astype(BF16)
+        out_ref[:, start : start + rows] = value.reshape(samples, rows, width)
+        start += rows
+    return start
+
+
+def pad_grads(out_ref, start):
+    samples, rows, width = out_ref.shape
+    if start < rows:
+        out_ref[:, start:] = jnp.zeros((samples, rows - start, width), BF16)
+
+
+def late_grads_kernel(
+    tcond, dtpre, dtin, single, dza, dzb, gated, dabranch, tinput, dfirst, dsecond, hidden,
+    dtbranch, out_ref,
+):
+    width = out_ref.shape[2]
+    start = store_grads(out_ref, 0, tcond[...], [dtpre[...], dtin[...]])
+    start = store_grads(out_ref, start, single[...], [dza[...], dzb[...]])
+    start = store_grads(out_ref, start, gated[...], [dabranch[...]])
+    halves = [
+        ref[:, lane : lane + width] for ref in (dfirst, dsecond) for lane in range(0, dfirst.shape[1], width)
     ]
+    start = store_grads(out_ref, start, tinput[...], halves)
+    start = store_grads(out_ref, start, hidden[...], [dtbranch[...]])
+    pad_grads(out_ref, start)
+
+
+def early_grads_kernel(
+    cond, dapre, dnormed, normed_in, dquery, dkeyval, dglogit, small_mid, small_last, pair_sum,
+    out_ref,
+):
+    samples, rows, width = out_ref.shape
+    start = store_grads(out_ref, 0, cond[...], [dapre[...], dnormed[...]])
+    start = store_grads(
+        out_ref, start, normed_in[...], [dquery[...], dkeyval[0], dkeyval[1], dglogit[...]]
+    )
+    pairs = jnp.concatenate(
+        [pair_sum[...], jnp.zeros((pair_sum.shape[0], width - pair_sum.shape[1]), F32)], axis=1
+    )
+    small = jnp.concatenate([small_mid[...], small_last[...], pairs], axis=0).astype(BF16)
+    for sample in range(samples):
+        out_ref[sample, start : start + small.shape[0]] = small
+    pad_grads(out_ref, start + small.shape[0])
+
+
+def grads_call(kernel, samples, rows, width, operands, name):
+    return pl.pallas_call(
+        kernel,
+        out_shape=jax.ShapeDtypeStruct((samples, rows, width), BF16),
+        compiler_params=params(),
+        name=name,
+    )(*operands)
+
+
+def pack_small(parts):
+    flat = jnp.concatenate([part.reshape(-1) for part in parts])
+    size = -(-flat.size // 4096) * 4096
+    return jnp.pad(flat, (0, size - flat.size)).reshape(1, size // 128, 128)
+
+
+def unpack_small(block, parts, axes):
+    samples = block.shape[0]
+    flat = block.reshape(samples, -1)
+    whole, start = [], 0
+    for part, axis in zip(parts, axes):
+        piece = flat[:, start : start + part.size].reshape((samples,) + part.shape)
+        start += part.size
+        piece = jnp.moveaxis(piece, 0, axis)
+        shape = list(part.shape)
+        shape[axis] *= samples
+        whole.append(piece.reshape(shape))
+    return whole
 
 
 def local(
@@ -559,67 +1245,76 @@
     zero_weight, zero_bias, attn_weight, query_bias, out_weight, pair_gain, pair_weight,
     trans_in, trans_out,
 ):
-    complexes, samples, rows_dev, width = tokens.shape
+    complexes, samples_own, rows_dev, width = tokens.shape
     narrow = single.shape[3]
     heads = pair_weight.shape[1]
-    length = pair.shape[2]
+    samples, chips = lax.axis_size("sample"), lax.axis_size("row") // 2
     own_start = (lax.axis_index("row") * rows_dev).astype(jnp.int32)
     meta = jnp.concatenate([own_start[None], token_count.astype(jnp.int32)])
-    full = gather_weights(
-        (cond_gain, ada_weight, ada_bias, zero_weight, zero_bias, attn_weight, query_bias,
-         out_weight, pair_gain, pair_weight, trans_in, trans_out),
-        (1, 1, 1, 1, 1, 1, 0, 0, 0, 0, 1, 0),
+
+    small_parts = (cond_gain, ada_bias, zero_bias, query_bias, pair_gain, pair_weight)
+    packed, ada, attn, zero, out_w, tin, tout = gather_weights(
+        [pack_small(small_parts), ada_weight, attn_weight, zero_weight, out_weight[None], trans_in,
+         trans_out[None]],
+        0,
     )
-    (gain, ada, ada_b, zero, zero_b, attn, query_b, out_w, pgain, pweight, tin, tout) = full
-    rows = complexes * samples * rows_dev
+    gain, ada_b, zero_b, query_b, pgain, pweight = unpack_small(packed, small_parts, (1, 1, 1, 0, 0, 0))
+
+    rows = complexes * samples_own * rows_dev
     flat = lambda value: value.reshape(rows, value.shape[-1])
-    block = lambda value: value.reshape(complexes, samples, rows_dev, width)
+    block = lambda value: value.reshape(complexes, samples_own, rows_dev, width)
     tok, sing, cot = flat(tokens), flat(single), flat(cotangent)
 
     pair_low, bias = pair_bias(meta, pair, pair_mask, pgain, pweight)
     normed_in, query, keyval, gate = project(tok, sing, gain, ada, ada_b, attn, query_b)
     query = block(query)
-    key_all = lax.all_gather(block(keyval[0]), "row", axis=2, tiled=True)
-    value_all = lax.all_gather(block(keyval[1]), "row", axis=2, tiled=True)
-    att, prob = attend(query, key_all, value_all, bias)
+    keyval = gather_rows(keyval.reshape(2, complexes, samples_own, rows_dev, width), 1)
+    att, prob = attend(query, keyval, bias)
     (
         output, dmid, datt, dglogit, gated, dabranch, dza, dzb, tcond, dtpre, dtin, tinput,
         dfirst, dsecond, hidden, dtbranch, small_mid,
     ) = middle_pass(
         meta, flat(att), gate, tok, sing, cot, gain, ada, ada_b, zero, zero_b, out_w, tin, tout,
-        complexes, samples, rows_dev,
+        complexes, samples_own, rows_dev,
     )
-    dquery, dkey, dvalue, dbias = attend_back(prob, block(datt), query, key_all, value_all)
-    dkey_own = lax.psum_scatter(dkey, "row", scatter_dimension=2, tiled=True)
-    dvalue_own = lax.psum_scatter(dvalue, "row", scatter_dimension=2, tiled=True)
+    dquery, dkeyval, dbias = attend_back(prob, block(datt), query, keyval)
+    dkeyval = reduce_rows(dkeyval, 2).reshape(2, rows, width)
     pair_sum = pair_grad(dbias, pair_low)
-    dquery, dkey_own, dvalue_own = flat(dquery), flat(dkey_own), flat(dvalue_own)
+    dquery = flat(dquery)
     tgrad, dnormed, dapre, cond, small_last = last_pass(
-        dquery, dkey_own, dvalue_own, dglogit, tok, sing, dmid, gain, ada, ada_b, attn
+        dquery, dkeyval, dglogit, tok, sing, dmid, gain, ada, ada_b, attn
     )
-    ada_grad = jnp.stack(weight_grad(cond, [dapre, dnormed]) + weight_grad(tcond, [dtpre, dtin]))
-    zero_grad = jnp.stack(weight_grad(sing, [dza, dzb]))
-    attn_grad = jnp.stack(weight_grad(normed_in, [dquery, dkey_own, dvalue_own, dglogit]))
-    out_grad = weight_grad(gated, [dabranch])[0]
-    tin_grad = jnp.stack(weight_grad(tinput, [dfirst, dsecond]))
-    tout_grad = weight_grad(hidden, [dtbranch])[0]
-
-    def reduce(value, axis):
-        part = lax.psum_scatter(value, "sample", scatter_dimension=axis, tiled=True)
-        return lax.psum(part, "row").astype(F32)
-
-    small = jnp.concatenate(
-        [small_mid.reshape(-1), small_last.reshape(-1), pair_sum.reshape(-1)]
+    slim, wide = narrow // samples, width // samples
+    late_parts = [slim] * 4 + [wide] * 5 + [tout.shape[2]]
+    early_parts = [slim] * 2 + [wide] * 4 + [16 + heads]
+    late = grads_call(
+        late_grads_kernel, samples, grad_rows(samples, chips, late_parts), width,
+        (tcond, dtpre, dtin, sing, dza, dzb, gated, dabranch, tinput, dfirst, dsecond, hidden, dtbranch),
+        "late_grads",
     )
-    small = lax.psum(small, ("row", "sample"))
-    mid_size = small_mid.size
-    small_mid = small[:mid_size].reshape(small_mid.shape)
-    small_last = small[mid_size : 2 * mid_size].reshape(small_last.shape)
-    pair_sum = small[2 * mid_size :].reshape(pair_sum.shape)
+    early = grads_call(
+        early_grads_kernel, samples, grad_rows(samples, chips, early_parts), width,
+        (cond, dapre, dnormed, normed_in, dquery, dkeyval, dglogit, small_mid, small_last, pair_sum),
+        "early_grads",
+    )
+    late = reduce_grads(late, 3)
+    early = reduce_grads(early, 4)
+
+    def pieces(total, parts):
+        out, start = [], 0
+        for size in parts:
+            out.append(total[start : start + size].astype(F32))
+            start += size
+        return out
+
+    late = pieces(late, late_parts)
+    early = pieces(early, early_parts)
+    small = early[6]
+    small_mid, small_last, pair_sum = small[:8], small[8:16], small[16:, : pair_weight.shape[0] * samples]
     spot = lax.axis_index("sample")
 
     def own_part(value, axis):
-        size = value.shape[axis] // lax.axis_size("sample")
+        size = value.shape[axis] // samples
         return lax.dynamic_slice_in_dim(value, spot * size, size, axis)
 
     gain_grad = own_part(jnp.stack([small_last[2, :narrow], small_mid[3, :narrow]]), 1)
@@ -634,17 +1329,17 @@
         output.reshape(tokens.shape),
         tgrad.reshape(tokens.shape),
         gain_grad,
-        reduce(ada_grad, 1),
+        jnp.stack([early[0], early[1], late[0], late[1]]),
         ada_bias_grad,
-        reduce(zero_grad, 1),
+        jnp.stack([late[2], late[3]]),
         zero_bias_grad,
-        reduce(attn_grad, 1),
+        jnp.stack(early[2:6]),
         query_bias_grad,
-        reduce(out_grad, 0),
+        late[4],
         pair_gain_grad,
         pair_weight_grad,
-        reduce(tin_grad, 1),
-        reduce(tout_grad, 0),
+        jnp.stack([jnp.concatenate(late[5:7], axis=1), jnp.concatenate(late[7:9], axis=1)]),
+        late[9],
     )
 
 

time: 942 us -> 622 us (0.66)
  waiting for transfers between devices: 671 us -> 0 us
  Pallas kernels: 114 us -> 588 us
  blocking collectives: 83 us -> 0 us
  between operations: 16.4 us -> 1.19 us
  matrix products: 15 us -> 0 us
    pallas_call x1 -> x8, Pallas kernels: 9.46 us -> 483 us  [the longest x2 204 us: reduce_grads(): pl.pallas_call(functools.partial(reduce_grads_kernel, chips, samples), in...]
    reduce_scatter x7 -> x0, waiting for transfers between devices: 322 us -> none  [the longest x5 233 us: reduce(): part = lax.psum_scatter(value, 'sample', scatter_dimension=axis, tiled=True)]
    all_gather x8 -> x0, waiting for transfers between devices: 269 us -> none  [the longest x6 213 us: gather_weights(): lax.all_gather(shard, 'sample', axis=axis, tiled=True)]
    psum x1 -> x0, blocking collectives: 41.3 us -> none  [local(): small = lax.psum(small, ('row', 'sample'))]
    psum x1 -> x0, waiting for transfers between devices: 40.1 us -> none  [reduce(): return lax.psum(part, 'row').astype(F32)]
    unnamed x18 -> x0, waiting for transfers between devices: 39.6 us -> none
    all_gather x4 -> x0, blocking collectives: 30.4 us -> none  [gather_weights(): lax.all_gather(shard, 'sample', axis=axis, tiled=True)]
    dot_general x14 -> x0, matrix products: 15 us -> none  [dot_tn(): lax.dot_general(left, right, (((0,), (0,)), ((), ())), preferred_element_...]
  transfers between devices with their start and end apart: 17 -> 0, of which waited for: 17 -> 0; matrix products, arithmetic and copies ran while one was open for 4% -> 0% of each run, Pallas kernels for 7% -> 0%
where the time goes in v2:
time: 622 us; the launch traced here: 617 us
  Pallas kernels  588 us (95%)
  local copies, waits for them, and re-layouts  15.1 us (2%)
  other arithmetic  12.4 us (2%)
    pallas_call x2, Pallas kernels, reduce_grads(): pl.pallas_call(functools.partial(reduce_grads_kernel, chips, samples), in...  204 us
    pallas_call x1, Pallas kernels, reduce_rows(): pl.pallas_call(functools.partial(reduce_rows_kernel, chips, samples), in_...  87.1 us
    pallas_call x1, Pallas kernels, gather_rows(): pl.pallas_call(functools.partial(gather_rows_kernel, chips, samples), in_...  86.1 us
    pallas_call x1, Pallas kernels, gather_weights(): pl.pallas_call(functools.partial(gather_kernel, count, chips, samples), i...  75.3 us
    pallas_call x1, Pallas kernels, pair_bias(): pl.pallas_call(pair_kernel, grid_spec=pltpu.PrefetchScalarGridSpec(num_sc...  27.2 us
    pallas_call x2, Pallas kernels, grads_call(): pl.pallas_call(kernel, out_shape=jax.ShapeDtypeStruct((samples, rows, wid...  21.5 us
    pallas_call x1, Pallas kernels, middle_pass(): pl.pallas_call(functools.partial(middle_kernel, samples, rows_dev), grid_...  21.2 us
    pallas_call x1, Pallas kernels, attend_back(): pl.pallas_call(functools.partial(attend_back_kernel, heads), grid=(comple...  20.1 us

profile of v2, /device:TPU:0, one launch (start us, length us, event | category | flops | bytes accessed | tf_op | source)
XLA Modules:
  0.0 616.9 jit_solution(3406304090251476828)
XLA Ops:
  0.6 0.8 copy.35
  1.4 0.1 reshape.119
  1.5 0.8 reshape.117
  2.3 0.8 reshape.118
  3.0 0.7 reshape.116
  3.8 1.4 concatenate.15
  5.2 0.6 pad_bitcast_fusion.refs_0_
  5.8 75.3 %gather_weights.1 = (bf16[4,1,32,128]{3,2,1,0:T(8,128)(2,1)}, bf16[4,4,96,768]{3,2,1,0:T(8,128)(2,1)}, bf16[4,4,192,768]{3,2,1,0:T(8,128)(2,1)}, bf16[4,2,96,768...) custom-call(bf16[1,32,128]{2,1,0:T(8,128)(2,1)} %pad_bitcast_fusion., ...), custom_call_target="tpu_custom_call" | custom-call | tf_op jit(solution)/shard_map/gather_weights/pallas_call | solution.py:379
  81.1 0.8 copy.45
  81.9 0.1 fusion.6
  82.0 0.1 reshape.124
  82.1 0.7 reshape.125.bias_ref.ada_bias_ref
  82.7 0.1 fusion.7
  82.8 0.1 reshape.122
  82.9 0.7 reshape.123.gain_ref
  83.6 0.7 reshape_reshape.6.qbias_ref
  84.2 8.5 %project.1 = (bf16[384,768]{1,0:T(8,128)(2,1)}, bf16[384,768]{1,0:T(8,128)(2,1)}, bf16[2,384,768]{2,1,0:T(8,128)(2,1)}, f32[384,768]{1,0:T(8,128)}) custom-call(bf16[384,768]{1,0:T(8,128)(2,1)} %bitcast.61, bf16[384,384]{1,0:T(8,128)(2,1)} %bitcast.64, bf16[2,384]{1,0:T(2,128)(2,1)} %reshape.123.gain_ref, bf16[4,4,96,768]{3,2,1,0:T(8,128)(2,1)} %get-tuple-element.55.ada_ref, ...), custom_call_target="tpu_custom_call" | custom-call | tf_op jit(solution)/shard_map/project/pallas_call | solution.py:812
  92.7 0.0 copy-start.1
  92.7 86.1 %gather_rows.1.keyval_ref = bf16[2,2,3,512,768]{4,3,2,1,0:T(8,128)(2,1)} custom-call(bf16[2,2,3,64,768]{4,3,2,1,0:T(8,128)(2,1)} %bitcast.73), custom_call_target="tpu_custom_call" | custom-call | tf_op jit(solution)/shard_map/gather_rows/pallas_call | solution.py:410
  178.8 0.1 slice.132
  178.9 0.1 reshape_reshape.7
  179.0 0.7 copy.38
  179.7 0.6 reshape.137.gain_ref
  180.3 0.0 copy-done.1
  180.3 0.6 pad_add_fusion.meta_ref
  180.8 27.2 %pair_bias.1 = (bf16[2,64,512,128]{3,2,1,0:T(8,128)(2,1)}, f32[2,16,64,512]{3,2,1,0:T(8,128)}) custom-call(s32[3]{0:T(128)} %pad_add_fusion.meta_ref, bf16[2,64,512,128]{3,2,1,0:T(8,128)(2,1)} %pair_ref.1, s32[2,64,512]{2,1,0:T(8,128)} %mask_ref.1, f32[1,128]{1,0:T(1,128)} %reshape.137.gain_ref, bf16[16,128]{1,0:T(8,128)(2,1)} %bitcast.82), custom_call_target="tpu_custom_call" | custom-call | tf_op jit(solution)/shard_map/pair_bias/pallas_call | solution.py:720
  208.0 13.0 %attend.1 = (f32[2,3,64,768]{3,2,1,0:T(8,128)}, bf16[2,3,16,64,512]{4,3,2,1,0:T(8,128)(2,1)}) custom-call(bf16[2,3,64,768]{3,2,1,0:T(8,128)(2,1)} %bitcast.68, bf16[2,2,3,512,768]{4,3,2,1,0:T(8,128)(2,1)} %gather_rows.1.keyval_ref, f32[2,16,64,512]{3,2,1,0:T(8,128)} %get-tuple-element.59.bias_ref), custom_call_target="tpu_custom_call" | custom-call | tf_op jit(solution)/shard_map/attend/pallas_call | solution.py:869
  220.9 0.1 reshape.130
  221.0 0.7 reshape.131.zero_bias_ref
  221.7 21.2 %middle_pass.1 = (bf16[384,768]{1,0:T(8,128)(2,1)}, f32[384,768]{1,0:T(8,128)}, bf16[384,768]{1,0:T(8,128)(2,1)}, bf16[384,768]{1,0:T(8,128)(2,1)}, bf16[384,768...) custom-call(s32[3]{0:T(128)} %pad_add_fusion.meta_ref, ...), custom_call_target="tpu_custom_call" | custom-call | tf_op jit(solution)/shard_map/middle_pass/pallas_call | solution.py:1048
  242.9 13.4 %late_grads.1.grads_ref = bf16[4,1792,768]{2,1,0:T(8,128)(2,1)} custom-call(bf16[384,384]{1,0:T(8,128)(2,1)} %get-tuple-element.82.tcond, bf16[384,768]{1,0:T(8,128)(2,1)} %get-tuple-element.83.dtpre, bf16[384,768]{1,0:T(8,128)(2,1)} %get-tuple-element.84.dtin, bf16[384,384]{1,0:T(8,128)(2,1)} %bitcast.66, bf16[384,768]{1,0:T(8,128)(2,1)} %get-tuple-element.85.dza, ...), custom_call_target="tpu_custom_call" | custom-call | tf_op jit(solution)/shard_map/late_grads/pallas_call | solution.py:1215
  256.2 123.3 %reduce_grads.3 = bf16[1792,768]{1,0:T(8,128)(2,1)} custom-call(bf16[4,1792,768]{2,1,0:T(8,128)(2,1)} %late_grads.1.grads_ref), custom_call_target="tpu_custom_call" | custom-call | tf_op jit(solution)/shard_map/reduce_grads/pallas_call | solution.py:633
  379.5 2.3 fusion.2
  381.8 0.1 maximum_bitcast_fusion
  381.9 1.6 maximum_convert_fusion.1
  383.4 20.1 %attend_back.1 = (bf16[2,3,64,768]{3,2,1,0:T(8,128)(2,1)}, bf16[2,2,3,512,768]{4,3,2,1,0:T(8,128)(2,1)}, f32[2,16,64,512]{3,2,1,0:T(8,128)}) custom-call(bf16[2,3,16,64,512]{4,3,2,1,0:T(8,128)(2,1)} %get-tuple-element.67.prob_ref, bf16[2,3,64,768]{3,2,1,0:T(8,128)(2,1)} %bitcast.75, bf16[2,3,64,768]{3,2,1,0:T(8,128)(2,1)} %bitcast.69, ...), custom_call_target="tpu_custom_call" | custom-call | tf_op jit(solution)/shard_map/attend_back/pallas_call | solution.py:929
  403.5 15.2 %pair_grad.1.pair_sum = f32[16,128]{1,0:T(8,128)} custom-call(f32[2,16,64,512]{3,2,1,0:T(8,128)} %get-tuple-element.80.dbias_ref, bf16[2,64,512,128]{3,2,1,0:T(8,128)(2,1)} %get-tuple-element.81.low_ref), custom_call_target="tpu_custom_call" | custom-call | tf_op jit(solution)/shard_map/pair_grad/pallas_call | solution.py:762
  418.7 87.1 %reduce_rows.1 = bf16[2,2,3,64,768]{4,3,2,1,0:T(8,128)(2,1)} custom-call(bf16[2,2,3,512,768]{4,3,2,1,0:T(8,128)(2,1)} %get-tuple-element.70.part_ref), custom_call_target="tpu_custom_call" | custom-call | tf_op jit(solution)/shard_map/reduce_rows/pallas_call | solution.py:505
  505.8 9.5 %last_pass.1 = (f32[384,768]{1,0:T(8,128)}, bf16[384,768]{1,0:T(8,128)(2,1)}, bf16[384,768]{1,0:T(8,128)(2,1)}, bf16[384,384]{1,0:T(8,128)(2,1)}, f32[8,768]{1,0:T(8,128)}) custom-call(bf16[384,768]{1,0:T(8,128)(2,1)} %bitcast.70, bf16[2,384,768]{2,1,0:T(8,128)(2,1)} %bitcast.59, bf16[384,768]{1,0:T(8,128)(2,1)} %get-tuple-element.71.dglogit_ref.dglogit, ...), custom_call_target="tpu_custom_call" | custom-call | tf_op jit(solution)/shard_map/last_pass/pallas_call | solution.py:1137
  515.4 8.2 %early_grads.1.grads_ref = bf16[4,1024,768]{2,1,0:T(8,128)(2,1)} custom-call(bf16[384,384]{1,0:T(8,128)(2,1)} %get-tuple-element.74.cond, bf16[384,768]{1,0:T(8,128)(2,1)} %get-tuple-element.75.dapre, bf16[384,768]{1,0:T(8,128)(2,1)} %get-tuple-element.76.dnormed, bf16[384,768]{1,0:T(8,128)(2,1)} %get-tuple-element.77.normed_in, bf16[384,768]{1,0:T(8,128)(2,1)} %bitcast.71, ...), custom_call_target="tpu_custom_call" | custom-call | tf_op jit(solution)/shard_map/early_grads/pallas_call | solution.py:1215
  523.5 0.0 copy-start
  523.5 80.5 %reduce_grads.2 = bf16[1024,768]{1,0:T(8,128)(2,1)} custom-call(bf16[4,1024,768]{2,1,0:T(8,128)(2,1)} %early_grads.1.grads_ref), custom_call_target="tpu_custom_call" | custom-call | tf_op jit(solution)/shard_map/reduce_grads/pallas_call | solution.py:633
  604.0 0.8 slice_convert_fusion.2
  604.8 0.0 copy-done
  604.8 0.1 reshape.138
  604.9 0.6 dynamic_slice.25
  605.5 1.3 slice_bitcast_fusion.3
  606.8 1.6 maximum_convert_fusion
  608.4 0.7 dynamic-slice_bitcast_fusion
  609.1 1.3 slice_bitcast_fusion.5
  610.4 0.9 maximum_convert_fusion.3
  611.3 0.7 fusion
  611.9 1.1 maximum_convert_fusion.2
  613.0 2.2 slice_convert_fusion
  615.2 0.6 constant_dynamic-slice_fusion
  615.8 0.6 fusion.1
  (9 shorter events, 0.1 us)
Async XLA Ops:
  92.7 87.5 %copy-start.1 = (s32[2]{0:T(128)S(1)}, s32[2]{0:T(128)}, u32[]{:S(2)}) copy-start(s32[2]{0:T(128)} %param.21) | copy-start | bytes 28
  523.5 81.3 %copy-start = (bf16[128,16]{0,1:T(8,128)(2,1)S(1)}, bf16[128,16]{0,1:T(8,128)(2,1)}, u32[]{:S(2)}) copy-start(bf16[128,16]{0,1:T(8,128)(2,1)} %copy.38) | copy-start | bytes 12292
